TPU v7x, 256 devices: a whole 4x4x8 slice. The times are simulated.
256 devices in a mesh: row: 4 (over x), col: 4 (over z_lo), leaf: 16 (over z_hi, y, core).
Axes of the slice: x: 4, y: 4, z: 8 (z_hi: 2, z_lo: 4; z = z_hi * 4 + z_lo), core: 2. Of those that a mesh axis runs over, the one named last changes fastest.
Arguments:
- copies: float32 [16, 3072, 3072], P('leaf', 'row', 'col'), may hold values from -4 to 4
- left_panels: bfloat16 [4, 2, 16, 3072, 1024], P(None, None, 'leaf', 'row', 'col'), may hold values from -6 to 6
- upper_panels: bfloat16 [4, 2, 16, 1024, 3072], P(None, None, 'leaf', 'row', 'col'), may hold values from -0.09375 to 0.09375
- live_blocks: int32 [4, 2, 16, 12], P(None, None, 'leaf'), may hold values from 0 to 23, as said below
Outputs:
- fronts: float32 [16, 3072, 3072], P('leaf', 'row', 'col')
Inputs may be any that keep to these rules, and one draw needn't show every extreme that they name: For each level l, node n and layer p, entries s * 3 to (s + 1) * 3 - 1 of live_blocks[l, n, p] are 3 distinct block numbers of slab s, that is, of s * 6 to (s + 1) * 6 - 1, in any order, for s from 0 to 3.
All inputs are finite; a program needn't handle non-finite values.
Results may differ from a plain program's by a relative error of at most 0.0003.
Values may be sent and summed in bfloat16 or wider, within the bound.
No kernel may reach another device: no remote copies, remote signals or barrier semaphores. Data moves between devices by JAX's collectives and lax.ppermute only.
A program may use at most 128 MiB of HBM per device.

v0:
```python
import jax
import jax.numpy as jnp
from jax import lax
from jax.sharding import PartitionSpec as P

BLK = 128


def from_partner(block, axis, bit):
    count = lax.axis_size(axis)
    route = []
    for low in range(count):
        high = low | 1 << bit
        if high != low and high < count:
            route += [(low, high), (high, low)]
    return lax.ppermute(block, axis, route)


def mask_of(block_ids, length):
    positions = jnp.arange(length, dtype=jnp.int32) // BLK
    hits = positions[None, None, :] == block_ids[:, :, None]
    return jnp.any(hits, axis=1).astype(jnp.bfloat16)


def on_device(copies, left_panels, upper_panels, live_blocks):
    current = copies[0]
    rows_dev, cols_dev = current.shape
    layer_id = lax.axis_index("leaf")
    row_id = lax.axis_index("row")
    col_id = lax.axis_index("col")
    row_count = lax.axis_size("row")
    leaf_count = lax.axis_size("leaf")
    half_count = live_blocks.shape[3] // row_count
    for height in range(left_panels.shape[0]):
        live_ids = live_blocks[height, :, 0, :]
        row_live = lax.dynamic_slice_in_dim(
            live_ids, row_id * half_count, half_count, 1
        ) - row_id * (rows_dev // BLK)
        col_live = lax.dynamic_slice_in_dim(
            live_ids, col_id * half_count, half_count, 1
        ) - col_id * (cols_dev // BLK)
        left_rows = left_panels[height, :, 0]
        upper_cols = upper_panels[height, :, 0]
        left_all = lax.all_gather(left_rows, "col", axis=2, tiled=True)
        upper_all = lax.all_gather(upper_cols, "row", axis=1, tiled=True)
        row_mask = mask_of(row_live, rows_dev)
        col_mask = mask_of(col_live, cols_dev)
        update = lax.dot_general(
            left_all * row_mask[:, :, None],
            upper_all * col_mask[:, None, :],
            (((0, 2), (0, 1)), ((), ())),
            preferred_element_type=jnp.float32,
        )
        active = layer_id % (1 << height) == 0
        current = jnp.where(active, current - update, current)
        upper_side = (layer_id >> height) % 2 == 1
        partner = from_partner(current, "leaf", height)
        joined = jnp.where(upper_side, partner + current, current + partner)
        current = jnp.where(active, joined, current)
    return current[None]


def solution(mesh):
    in_specs = (
        P("leaf", "row", "col"),
        P(None, None, "leaf", "row", "col"),
        P(None, None, "leaf", "row", "col"),
        P(None, None, "leaf", None),
    )
    out_specs = P("leaf", "row", "col")
    return jax.shard_map(
        on_device, mesh=mesh, in_specs=in_specs, out_specs=out_specs, check_vma=False
    )
```

profile of v0, /device:TPU:3, one launch (start us, length us, event | category | flops | bytes accessed | tf_op | source)
XLA Modules:
  0.0 588.1 jit_solution(13897013917587618549)
XLA Ops:
  6.5 0.0 all-gather.19.cloned.1.call-start
  6.5 3.7 fusion.25
  10.2 0.0 all-gather.19.cloned.1.call-update
  10.3 0.0 all-gather.17.cloned.1.call-start
  10.3 0.0 copy-done
  10.3 1.8 fusion.24
  12.1 0.0 all-gather.17.cloned.1.call-update
  12.1 0.0 all-gather.23.cloned.1.call-start
  12.2 0.7 all-gather.23.cloned.1.call-update
  12.9 0.0 all-gather.21.cloned.1.call-start
  12.9 0.5 all-gather.21.cloned.1.call-update
  13.5 0.0 all-gather.27.cloned.1.call-start
  13.5 0.5 all-gather.27.cloned.1.call-update
  14.0 0.0 all-gather.25.cloned.1.call-start
  14.1 0.5 all-gather.25.cloned.1.call-update
  14.6 0.0 all-gather.31.cloned.1.call-start
  14.7 0.7 all-gather.31.cloned.1.call-update
  15.4 0.0 all-gather.29.cloned.1.call-start
  15.4 0.0 copy-done.2
  15.5 0.1 fusion.21
  15.5 0.1 fusion.16
  15.6 0.2 compare_reduce_fusion.1
  15.9 38.6 %all-gather.19.cloned.1.call-done = bf16[1,2,1,1024,768]{4,3,2,1,0:T(8,128)(2,1)} async-done(((bf16[1,2,1,256,768]{4,3,2,1,0:T(8,128)(2,1)}), bf16[1,2,1,1024,768]{4,3,2,1,0:T(8,128)(2,1)}) %all-gather.19.cloned.1.call-update) | async-done | bytes 3145744 | tf_op jit(solution)/shard_map/all_gather | solution.py:45
  54.4 72.7 %all-gather.17.cloned.1.call-done = bf16[1,2,1,768,1024]{4,3,2,1,0:T(8,128)(2,1)} async-done(((bf16[1,2,1,768,256]{4,3,2,1,0:T(8,128)(2,1)}), bf16[1,2,1,768,1024]{4,3,2,1,0:T(8,128)(2,1)}) %all-gather.17.cloned.1.call-update) | async-done | bytes 3145744 | tf_op jit(solution)/shard_map/all_gather | solution.py:44
  127.1 6.9 %bitcast_subtract_fusion = f32[768,768]{1,0:T(8,128)} fusion(f32[1,768,768]{2,1,0:T(8,128)S(1)} %copy-done.3, bf16[1,2,1,1024,768]{4,3,2,1,0:T(8,128)(2,1)} %all-gather.19.cloned.1.call-done, bf16[1,2,1,768,1024]{4,3,2,1,0:T(8,128)(2,1)} %all-gather.17.cloned.1.call-done, bf16[2,768]{1,0:T(2,128)(2,1)S(1)} %convert_element_type.57, ...), kind=kOutput, calls=%fused_computation.19 | convolution fusion | flops 2419654656 | bytes 11016192 | tf_op jit(solution)/shard_map/dot_general | solution.py:48
  134.0 0.5 collective-permute-start
  134.6 0.0 all-gather.29.cloned.1.call-update
  134.6 32.4 %all-gather.23.cloned.1.call-done = bf16[1,2,1,1024,768]{4,3,2,1,0:T(8,128)(2,1)} async-done(((bf16[1,2,1,256,768]{4,3,2,1,0:T(8,128)(2,1)}), bf16[1,2,1,1024,768]{4,3,2,1,0:T(8,128)(2,1)}) %all-gather.23.cloned.1.call-update) | async-done | bytes 3145744 | tf_op jit(solution)/shard_map/all_gather | solution.py:45
  167.1 72.5 %all-gather.21.cloned.1.call-done = bf16[1,2,1,768,1024]{4,3,2,1,0:T(8,128)(2,1)} async-done(((bf16[1,2,1,768,256]{4,3,2,1,0:T(8,128)(2,1)}), bf16[1,2,1,768,1024]{4,3,2,1,0:T(8,128)(2,1)}) %all-gather.21.cloned.1.call-update) | async-done | bytes 3145744 | tf_op jit(solution)/shard_map/all_gather | solution.py:44
  239.6 0.0 collective-permute-done
  239.6 6.8 %subtract_select_fusion.2 = f32[768,768]{1,0:T(8,128)S(1)} fusion(f32[768,768]{1,0:T(8,128)} %collective-permute-done, f32[768,768]{1,0:T(8,128)} %bitcast_subtract_fusion, bf16[1,2,1,1024,768]{4,3,2,1,0:T(8,128)(2,1)} %all-gather.23.cloned.1.call-done, bf16[1,2,1,768,1024]{4,3,2,1,0:T(8,128)(2,1)} %all-gather.21.cloned.1.call-done, ...), kind=kOutput, calls=%fused_computation.5 | convolution fusion | flops 2420834304 | bytes 13375489 | tf_op jit(solution)/shard_map/dot_general | solution.py:48
  246.5 0.0 copy-start.1
  246.5 1.3 collective-permute-start.1
  247.8 31.6 %all-gather.27.cloned.1.call-done = bf16[1,2,1,1024,768]{4,3,2,1,0:T(8,128)(2,1)} async-done(((bf16[1,2,1,256,768]{4,3,2,1,0:T(8,128)(2,1)}), bf16[1,2,1,1024,768]{4,3,2,1,0:T(8,128)(2,1)}) %all-gather.27.cloned.1.call-update) | async-done | bytes 3145744 | tf_op jit(solution)/shard_map/all_gather | solution.py:45
  279.4 72.5 %all-gather.25.cloned.1.call-done = bf16[1,2,1,768,1024]{4,3,2,1,0:T(8,128)(2,1)} async-done(((bf16[1,2,1,768,256]{4,3,2,1,0:T(8,128)(2,1)}), bf16[1,2,1,768,1024]{4,3,2,1,0:T(8,128)(2,1)}) %all-gather.25.cloned.1.call-update) | async-done | bytes 3145744 | tf_op jit(solution)/shard_map/all_gather | solution.py:44
  351.9 5.5 fusion.1
  357.4 0.0 copy-done.1
  357.4 0.0 collective-permute-done.1
  357.4 2.8 subtract_select_fusion.1
  360.3 3.0 collective-permute-start.2
  363.3 28.6 %all-gather.31.cloned.1.call-done = bf16[1,2,1,1024,768]{4,3,2,1,0:T(8,128)(2,1)} async-done(((bf16[1,2,1,256,768]{4,3,2,1,0:T(8,128)(2,1)}), bf16[1,2,1,1024,768]{4,3,2,1,0:T(8,128)(2,1)}) %all-gather.31.cloned.1.call-update) | async-done | bytes 3145744 | tf_op jit(solution)/shard_map/all_gather | solution.py:45
  391.9 72.7 %all-gather.29.cloned.1.call-done = bf16[1,2,1,768,1024]{4,3,2,1,0:T(8,128)(2,1)} async-done(((bf16[1,2,1,768,256]{4,3,2,1,0:T(8,128)(2,1)}), bf16[1,2,1,768,1024]{4,3,2,1,0:T(8,128)(2,1)}) %all-gather.29.cloned.1.call-update) | async-done | bytes 3145744 | tf_op jit(solution)/shard_map/all_gather | solution.py:44
  464.6 5.5 fusion
  470.0 0.0 collective-permute-done.2
  470.1 2.3 subtract_select_fusion
  472.3 1.4 collective-permute-start.3
  473.7 105.8 %collective-permute-done.3 = f32[768,768]{1,0:T(8,128)S(1)} collective-permute-done((f32[768,768]{1,0:T(8,128)S(1)}, f32[768,768]{1,0:T(8,128)S(1)}, u32[]{:S(2)}, u32[]{:S(2)}) %collective-permute-start.3) | collective-permute-done | bytes 2359328 | tf_op jit(solution)/shard_map/ppermute | solution.py:16
  579.6 1.7 fusion.4
  (14 shorter events, 0.1 us)
Async XLA Ops:
  6.5 3.8 copy-start
  6.5 47.9 %all-gather.19.cloned.1.call-start = ((), (), s32[]{:S(2)}) async-start(), calls=%async_computation.1 | async-start | bytes 3932160 | tf_op jit(solution)/shard_map/all_gather | solution.py:45
  10.3 116.8 %all-gather.17.cloned.1.call-start = ((), (), s32[]{:S(2)}) async-start(), calls=%async_computation | async-start | bytes 3932160 | tf_op jit(solution)/shard_map/all_gather | solution.py:44
  12.1 3.3 copy-start.2
  12.1 115.0 %copy-start.3 = (f32[1,768,768]{2,1,0:T(8,128)S(1)}, f32[1,768,768]{2,1,0:T(8,128)}, u32[]{:S(2)}) copy-start(f32[1,768,768]{2,1,0:T(8,128)} %param.4) | copy-start | bytes 7077892
  12.1 154.9 %all-gather.23.cloned.1.call-start = ((), (), s32[]{:S(2)}) async-start(), calls=%async_computation.3 | async-start | bytes 3932160 | tf_op jit(solution)/shard_map/all_gather | solution.py:45
  12.9 226.7 %all-gather.21.cloned.1.call-start = ((), (), s32[]{:S(2)}) async-start(), calls=%async_computation.2 | async-start | bytes 3932160 | tf_op jit(solution)/shard_map/all_gather | solution.py:44
  13.5 266.0 %all-gather.27.cloned.1.call-start = ((), (), s32[]{:S(2)}) async-start(), calls=%async_computation.5 | async-start | bytes 3932160 | tf_op jit(solution)/shard_map/all_gather | solution.py:45
  14.0 337.9 %all-gather.25.cloned.1.call-start = ((), (), s32[]{:S(2)}) async-start(), calls=%async_computation.4 | async-start | bytes 3932160 | tf_op jit(solution)/shard_map/all_gather | solution.py:44
  14.6 377.3 %all-gather.31.cloned.1.call-start = ((), (), s32[]{:S(2)}) async-start(), calls=%async_computation.7 | async-start | bytes 3932160 | tf_op jit(solution)/shard_map/all_gather | solution.py:45
  15.4 449.2 %all-gather.29.cloned.1.call-start = ((), (), s32[]{:S(2)}) async-start(), calls=%async_computation.6 | async-start | bytes 3932160 | tf_op jit(solution)/shard_map/all_gather | solution.py:44
  134.0 105.6 %collective-permute-start = (f32[768,768]{1,0:T(8,128)}, f32[768,768]{1,0:T(8,128)}, u32[]{:S(2)}, u32[]{:S(2)}) collective-permute-start(f32[768,768]{1,0:T(8,128)} %bitcast_subtract_fusion), channel_id=1, source_target_pairs={{0,1},{1,0},{2,3},{3,2},{4,5},{5,4},{6,7},{7,6},{8,9},{9,8},{10,11... | collective-permute-start | bytes 7077896 | tf_op jit(solution)/shard_map/ppermute | solution.py:16
  246.5 111.0 %copy-start.1 = (f32[768,768]{1,0:T(8,128)}, f32[768,768]{1,0:T(8,128)S(1)}, u32[]{:S(2)}) copy-start(f32[768,768]{1,0:T(8,128)S(1)} %subtract_select_fusion.2) | copy-start | bytes 7077892
  246.5 111.0 %collective-permute-start.1 = (f32[768,768]{1,0:T(8,128)S(1)}, f32[768,768]{1,0:T(8,128)}, u32[]{:S(2)}, u32[]{:S(2)}) collective-permute-start(f32[768,768]{1,0:T(8,128)S(1)} %subtract_select_fusion.2), channel_id=1, source_target_pairs={{0,2},{2,0},{1,3},{3,1},{4,6},{6,4},{5,7},{7,5},{8,10},{10,8},{9,1... | collective-permute-start | bytes 7077896 | tf_op jit(solution)/shard_map/ppermute | solution.py:16
  360.3 109.8 %collective-permute-start.2 = (f32[768,768]{1,0:T(8,128)S(1)}, f32[768,768]{1,0:T(8,128)}, u32[]{:S(2)}, u32[]{:S(2)}) collective-permute-start(f32[768,768]{1,0:T(8,128)S(1)} %subtract_select_fusion.1), channel_id=1, source_target_pairs={{0,4},{4,0},{1,5},{5,1},{2,6},{6,2},{3,7},{7,3},{8,12},{12,8},{9,1... | collective-permute-start | bytes 7077896 | tf_op jit(solution)/shard_map/ppermute | solution.py:16
  472.3 107.3 %collective-permute-start.3 = (f32[768,768]{1,0:T(8,128)S(1)}, f32[768,768]{1,0:T(8,128)S(1)}, u32[]{:S(2)}, u32[]{:S(2)}) collective-permute-start(f32[768,768]{1,0:T(8,128)S(1)} %subtract_select_fusion), channel_id=1, source_target_pairs={{0,8},{8,0},{1,9},{9,1},{2,10},{10,2},{3,11},{11,3},{4,12},{12,4},... | collective-permute-start | bytes 7077896 | tf_op jit(solution)/shard_map/ppermute | solution.py:16
Sparse Core Ops, SparseCore 0:
  10.4 44.0 all-gather.18
  56.2 70.8 all-gather.16
  128.9 38.1 all-gather.22
  168.7 70.8 all-gather.20
  241.2 38.1 all-gather.26
  281.1 70.8 all-gather.24
  353.7 38.1 all-gather.30
  393.7 70.8 all-gather.28
where the time goes:
time: 588 us
  waiting for transfers between devices  530 us (90%)
  matrix products  24.7 us (4%)
  between operations  13.7 us (2%)
  other arithmetic  7.24 us (1%)
  starting transfers between devices  6.53 us (1%)
    all_gather x4, waiting for transfers between devices, on_device(): left_all = lax.all_gather(left_rows, 'col', axis=2, tiled=True)  290 us
    all_gather x4, waiting for transfers between devices, on_device(): upper_all = lax.all_gather(upper_cols, 'row', axis=1, tiled=True)  131 us
    ppermute x4, waiting for transfers between devices, from_partner(): return lax.ppermute(block, axis, route)  106 us
    dot_general x4, matrix products, on_device(): lax.dot_general(left_all * row_mask[:, :, None], upper_all * col_mask[:,...  24.7 us
  transfers between devices with their start and end apart: 12, of which 9 were waited for; matrix products, arithmetic and copies ran while one was open for 5% of the time, Pallas kernels for 0%

commit v1 on v0

v1 whole, which is shorter than its diff:
```python
import functools

import jax
import jax.numpy as jnp
from jax import lax
from jax.experimental import pallas as pl
from jax.experimental.pallas import tpu as pltpu
from jax.sharding import PartitionSpec as P


AXES = ("row", "col", "leaf")
SIDE = 4
LEAF = 16
BLK = 128
LIVE = 3
SLAB = 6
NODES = 2
KC = 256
BF = jnp.bfloat16
F32 = jnp.float32
ORDER = (0, 2, 1, 3)
ANY = pl.BlockSpec(memory_space=pl.ANY)
VMEM = pl.BlockSpec(memory_space=pltpu.VMEM)
HBM = pl.BlockSpec(memory_space=pltpu.HBM)
SMEM = pl.BlockSpec(memory_space=pltpu.SMEM)

L1, L2, L3, U = 2 * LIVE * BLK, 2 * LIVE * 64, 2 * LIVE * 32, LIVE * KC
NUM = 16
AT_L2 = (L1, L1 + L2)
AT_L3 = tuple(L1 + 2 * L2 + j * L3 for j in range(4))
AT_U = tuple(L1 + 2 * L2 + 4 * L3 + j * U for j in range(3))
AT_NUM = AT_U[2] + U
PACK = AT_NUM + NUM


def send(x, move):
    pairs = []
    for r in range(SIDE):
        for c in range(SIDE):
            for p in range(LEAF):
                to = move(r, c, p)
                if to is not None:
                    flat = [(a * SIDE + b) * LEAF + d for a, b, d in ((r, c, p), to)]
                    pairs.append(tuple(flat))
    return lax.ppermute(x, AXES, pairs)


def flip_leaf(bits):
    return lambda r, c, p: (r, c, p ^ bits)


def gather(left, upper):
    lefts, uppers = [left], [upper]
    for e in ORDER[1:]:
        lefts.append(send(left, lambda r, c, p: (r, c ^ e, p)))
        uppers.append(send(upper, lambda r, c, p: (r ^ e, c, p)))
    return lefts, uppers


def start_all(copies, sem):
    for src, dst in copies:
        pltpu.make_async_copy(src, dst, sem).start()


def wait_for(ref, sem):
    pltpu.make_async_copy(ref, ref, sem).wait()


def live_block(ids, level, n, slab, i):
    return ids[level, n, slab * LIVE + i] - slab * SLAB


def pack0_kernel(ids, role, left, upper, lo, uo, sems):
    for n in range(NODES):
        for i in range(LIVE):
            rb = pl.multiple_of(live_block(ids, 0, n, role[0], i) * BLK, BLK)
            cb = pl.multiple_of(live_block(ids, 0, n, role[1], i) * BLK, BLK)
            lefts = [(left.at[0, n, 0, pl.ds(rb, BLK), pl.ds(k * 128, 128)], lo.at[n, k, pl.ds(i * BLK, BLK)]) for k in range(2)]
            start_all(lefts, sems.at[0])
            start_all([(upper.at[0, n, 0, :, pl.ds(cb, BLK)], uo.at[n, i])], sems.at[1])
    wait_for(lo, sems.at[0])
    wait_for(uo, sems.at[1])


def pack123_kernel(ids, role, left, upper, w0, w1, nums, sems):
    lane = lax.broadcasted_iota(jnp.int32, (NUM, 128), 1)
    row = jnp.zeros((NUM, 128), F32)
    for level in (1, 2, 3):
        for n in range(NODES):
            for i in range(SIDE * LIVE):
                at = ((level - 1) * NODES + n) * SIDE * LIVE + i
                row = jnp.where(lane == at, ids[level, n, i].astype(F32), row)
    nums[...] = row.astype(BF)
    for n, out in ((1, w1), (0, w0)):
        copies = []
        for i in range(LIVE):
            for level in (1, 2, 3):
                rb = live_block(ids, level, n, role[0], i) * BLK
                for k in range(2):
                    half = pl.ds(k * 128, 128)

                    def piece(offset, rows, at):
                        src = left.at[level, n, 0, pl.ds(pl.multiple_of(rb + offset, rows), rows), half]
                        copies.append((src, out.at[pl.ds(at, rows)]))

                    if level == 1:
                        piece(0, BLK, (k * LIVE + i) * BLK)
                    for core in range(2):
                        if level == 2:
                            for s1 in range(2):
                                piece(core * 64 + s1 * 32, 32, AT_L2[s1] + (k * LIVE + i) * 64 + core * 32)
                        if level == 3:
                            for y in range(4):
                                piece(
                                    core * 64 + y % 2 * 32 + y // 2 * 16, 16, AT_L3[y] + (k * LIVE + i) * 32 + core * 16
                                )
                cb = pl.multiple_of(live_block(ids, level, n, role[1], i) * BLK, BLK)
                copies.append((upper.at[level, n, 0, :, pl.ds(cb, BLK)], out.at[pl.ds(AT_U[level - 1] + i * KC, KC)]))
        copies.append((nums, out.at[pl.ds(AT_NUM, NUM)]))
        start_all(copies, sems.at[n])
    wait_for(w1, sems.at[1])
    wait_for(w0, sems.at[0])


def take(src, parts, sem):
    for a, dst, b, size in parts:
        pltpu.make_async_copy(src.at[pl.ds(a, size)], dst.at[pl.ds(b, size)], sem).start()


def deal_kernel(role, w0, w1, m1, m2, m3, lo, uo, own, sems):
    parts = [(0, lo, 0, L1), (AT_U[0], uo, 0, U)]
    for y, out in ((1, m1), (2, m2), (3, m3), (0, own)):
        at = 0
        pieces = [(AT_L3[y], L3), (AT_U[2], U), (AT_NUM, NUM)]
        if y < 2:
            pieces = [(AT_L2[y], L2), (AT_U[1], U)] + pieces
        for a, size in pieces:
            parts.append((a, out, at, size))
            at += size
    for core, src in ((0, w0), (1, w1)):
        pl.when(role[2] == core)(functools.partial(take, src, parts, sems.at[0]))
    for out in (m1, m2, m3, lo, uo, own):
        wait_for(out, sems.at[0])


def choose_kernel(role, own, m1, m2, m3, zo, xo, nums, sem):
    y = role[3]
    two = ((0, zo, 0, L2), (L2, xo, 0, U), (L2 + U + L3 + U, nums, NUM, NUM))
    three = ((L2 + U, zo, L2, L3), (L2 + U + L3, xo, U, U), (L2 + U + L3 + U, nums, 2 * NUM, NUM))
    three_m = ((0, zo, L2, L3), (L3, xo, U, U), (L3 + U, nums, 2 * NUM, NUM))
    take(own, ((L2 + U + L3 + U, nums, 0, NUM),), sem)
    for odd, src in ((0, own), (1, m1)):
        pl.when(y % 2 == odd)(functools.partial(take, src, two, sem))
    for at, src, parts in ((0, own, three), (1, m1, three), (2, m2, three_m), (3, m3, three_m)):
        pl.when(y == at)(functools.partial(take, src, parts, sem))
    for out in (zo, xo, nums):
        wait_for(out, sem)


def load_panels(role, lefts, uppers, rows, l_at, u_at, la, ua, sem):
    copies = []
    for e in range(SIDE):
        lj = pl.multiple_of((role[1] ^ ORDER[e]) * KC, KC)
        uj = pl.multiple_of((role[0] ^ ORDER[e]) * KC, KC)
        for k in range(2):
            src = lefts[e].at[pl.ds(l_at + k * rows, rows)]
            copies.append((src, la.at[:, pl.ds(lj + k * 128, 128)]))
        for i in range(LIVE):
            src = uppers[e].at[pl.ds(u_at + i * KC, KC)]
            copies.append((src, ua.at[pl.ds(uj, KC), pl.ds(i * BLK, BLK)]))
    start_all(copies, sem)


def subtract(ids, role, level, n, rows, c, out):
    for i in range(LIVE):
        rb = pl.multiple_of(live_block(ids, level, n, role[0], i) * rows, rows)
        for j in range(LIVE):
            cb = pl.multiple_of(live_block(ids, level, n, role[1], j) * BLK, BLK)
            out[pl.ds(rb, rows), pl.ds(cb, BLK)] -= c[i * rows : (i + 1) * rows, j * BLK : (j + 1) * BLK]


def run_of(t, b, rows, which):
    return t[pl.ds(pl.multiple_of(b * 2 * rows + which * rows, rows), rows)]


def split(t, keep, give, rows, which):
    for b in range(SLAB):
        keep[pl.ds(b * rows, rows)] = run_of(t, b, rows, which)
        give[pl.ds(b * rows, rows)] = run_of(t, b, rows, 1 - which)


def split_coded(t, keep, give, rows, which):
    for b in range(SLAB):
        keep[pl.ds(b * rows, rows)] = run_of(t, b, rows, which)
        encode(run_of(t, b, rows, 1 - which), give.at[pl.ds(b * rows, rows)])


def encode(x, out):
    top = jnp.max(jnp.abs(x), axis=1, keepdims=True)
    e = jnp.floor(8.0 * jnp.log2(jnp.maximum(top, 1e-25)) + 0.04) - 119.0
    width = x.shape[1]
    out[:, :width] = jnp.round(x * jnp.exp2(-0.125 * e)).astype(jnp.int32).astype(jnp.int16)
    out[:, width:] = jnp.broadcast_to(e, (x.shape[0], 128)).astype(jnp.int32).astype(jnp.int16)


def decode(q):
    width = q.shape[1] - 128
    step = jnp.exp2(0.125 * q[:, width:].astype(jnp.int32).astype(F32))
    parts = [q[:, j * 128 : (j + 1) * 128].astype(jnp.int32).astype(F32) * step for j in range(width // 128)]
    return jnp.concatenate(parts, axis=1)


def update0_kernel(ids, role, front, *refs):
    lefts, uppers, (out, la, ua, sem) = refs[:4], refs[4:8], refs[8:]
    rows = LIVE * BLK
    for n in range(NODES):
        load_panels(role, lefts, uppers, rows, n * 2 * rows, n * LIVE * KC, la.at[n], ua.at[n], sem)
    out[...] = front[...]
    wait_for(la, sem)
    wait_for(ua, sem)
    for n in range(NODES):
        c = jnp.dot(la[n], ua[n], preferred_element_type=F32)
        subtract(ids, role, 0, n, BLK, c, out)


def update1_kernel(ids, role, t0, *refs):
    lefts, uppers, (keep, give, la, ua, t, sem) = refs[:4], refs[4:8], refs[8:]
    load_panels(role, lefts, uppers, LIVE * BLK, 0, 0, la, ua, sem)
    t[...] = t0[...]
    wait_for(la, sem)
    wait_for(ua, sem)
    c = jnp.dot(la[...], ua[...], preferred_element_type=F32)
    subtract(ids, role, 1, role[2], BLK, c, t)
    split(t, keep, give, 64, role[2])


def join_kernel(role, mine, theirs, keep, give, t):
    t[...] = mine[...] + theirs[...]
    split_coded(t, keep, give, 32, role[3] % 2)


def product23_kernel(role, *refs):
    lefts, uppers, (mine, other, la2, ua2, la3, ua3, sems) = refs[:4], refs[4:8], refs[8:]
    load_panels(role, lefts, uppers, LIVE * 64, 0, 0, la2, ua2, sems.at[0])
    load_panels(role, lefts, uppers, LIVE * 32, L2, U, la3, ua3, sems.at[1])
    at = 0
    for rows, la, ua, sem in ((32, la2, ua2, sems.at[0]), (16, la3, ua3, sems.at[1])):
        wait_for(la, sem)
        wait_for(ua, sem)
        c = jnp.dot(la[...], ua[...], preferred_element_type=F32)
        for i in range(LIVE):
            a, b = (c[(2 * i + k) * rows : (2 * i + k + 1) * rows] for k in range(2))
            first = role[2] == 0
            here = pl.ds(at + i * rows, rows)
            mine[here] = jnp.where(first, a, b)
            other[here] = jnp.where(first, b, a)
        at += LIVE * rows


def subtract_both(ids, role, level, at, rows, mine, theirs, t):
    here = pl.ds(at, LIVE * rows)
    subtract(ids, role, level, role[2], rows, mine[here], t)
    subtract(ids, role, level, 1 - role[2], rows, theirs[here], t)


def update2_kernel(ids, role, a, b, mine, theirs, s, sq, keep, give, t):
    total = a[...] + decode(b[...])
    s[...] = total
    t[...] = total
    subtract_both(ids, role, 2, 0, 32, mine, theirs, t)
    split_coded(t, keep, give, 16, role[3] // 2)
    encode(total, sq)


def update3_kernel(ids, role, a, b, mine, theirs, s, sq, t, tq):
    total = a[...] + decode(b[...])
    s[...] = total
    t[...] = total
    subtract_both(ids, role, 3, LIVE * 32, 16, mine, theirs, t)
    encode(t[...], tq)
    encode(total, sq)


def last_kernel(t, r, f, fq):
    total = t[...] + decode(r[...])
    f[...] = total
    encode(total, fq)


def collect_kernel(role, s1, r1, s2, *refs):
    eighths, (out, sem) = refs[:3], refs[3:]
    for odd, srcs in ((1, (s1, r1)), (0, (s2,) + eighths)):
        rows = srcs[0].shape[0]
        parts = [(src, ((0, out, j * rows, rows),)) for j, src in enumerate(srcs)]

        @pl.when(role[3] % 2 == odd)
        def _():
            for src, where in parts:
                take(src, where, sem)
    wait_for(out, sem)


def finish_kernel(role, t0, r0, s1, r1, s2, *refs):
    e2, c12, f8, e3, c3, (out, whole, buf, codes, sems) = refs[:3], refs[3], refs[4], refs[5:8], refs[8:12], refs[12:]
    core, y = role[2], role[3]

    def put(rows, where, own, own_at, coded):
        n = SLAB * rows
        mine = pltpu.make_async_copy(own, buf.at[pl.ds(0, n)], sems.at[1])
        mine.start()
        for j, (src, at) in enumerate(coded):
            pltpu.make_async_copy(src.at[pl.ds(at, n)], codes.at[pl.ds(j * n, n)], sems.at[0]).start()
        wait_for(codes.at[pl.ds(0, len(coded) * n)], sems.at[0])
        for j, first in enumerate(where):
            for b in range(SLAB):
                whole[pl.ds(b * BLK + first, rows)] = decode(codes[pl.ds(j * n + b * rows, rows)])
        mine.wait()
        for b in range(SLAB):
            whole[pl.ds(b * BLK + own_at, rows)] = buf[pl.ds(b * rows, rows)]
        flush()

    def flush():
        c = pltpu.make_async_copy(whole, out, sems.at[2])
        c.start()
        c.wait()

    @pl.when(core == 1)
    def _():
        a = pltpu.make_async_copy(t0, whole, sems.at[0])
        b = pltpu.make_async_copy(r0, buf, sems.at[1])
        a.start()
        b.start()
        a.wait()
        b.wait()
        whole[...] += buf[...]
        flush()

    @pl.when((core == 0) & (y % 2 == 1))
    def _():
        n = SLAB * 32
        put(32, (0, 96, 64), s1, 32, [(r1, 0), (c12, 0), (c12, n)])

    def eighths(own, own_y, coded):
        ys = [y ^ own_y for y in (1, 2, 3)]
        row = lambda y: y % 2 * 32 + y // 2 * 16
        put(16, [row(y) for y in ys] + [64 + row(y) for y in [own_y] + ys], own, row(own_y), coded)

    n = SLAB * 16
    pl.when((core == 0) & (y == 2))(
        lambda: eighths(s2, 2, [(r, 0) for r in e2] + [(c12, j * n) for j in range(4)])
    )
    pl.when((core == 0) & (y == 0))(
        lambda: eighths(f8, 0, [(r, 0) for r in e3] + [(r, 0) for r in c3])
    )


def grant(mib):
    return pltpu.CompilerParams(vmem_limit_bytes=mib << 20)


def sds(*shape, dtype=BF):
    return jax.ShapeDtypeStruct(shape, dtype)


def call(kernel, specs, outs, scratch, mib, *args, out_spec=VMEM):
    return pl.pallas_call(
        kernel,
        out_shape=outs,
        in_specs=specs,
        out_specs=jax.tree.map(lambda _: out_spec, outs),
        scratch_shapes=scratch,
        compiler_params=None if mib is None else grant(mib),
        cost_estimate=pl.CostEstimate(flops=1 << 30, bytes_accessed=4 << 20, transcendentals=0),
    )(*args)


def on_device(copies, left, upper, live):
    row, col, leaf = (lax.axis_index(a) for a in AXES)
    role = jnp.stack([row, col, leaf % 2, leaf // 2 % 4]).astype(jnp.int32)
    ids0 = live[:, :, 0, :]
    front = copies[0]
    cols = front.shape[1]
    dma = pltpu.SemaphoreType.DMA
    inner = SIDE * KC

    def f32(rows, width=cols):
        return sds(rows, width, dtype=F32)

    def codes(rows):
        return sds(rows, cols + 128, dtype=jnp.int16)

    def panels(rows):
        return [pltpu.VMEM((rows, inner), BF), pltpu.VMEM((inner, LIVE * BLK), BF)]

    lp0, up0 = call(
        pack0_kernel, [SMEM, SMEM, HBM, HBM],
        (sds(NODES, 2, LIVE * BLK, 128), sds(NODES, LIVE, KC, BLK)), [dma((2,))], None,
        ids0, role, left, upper,
    )
    left, upper, lp0, up0 = lax.optimization_barrier((left, upper, lp0.reshape(-1, 128), up0.reshape(-1, 128)))
    l0, u0 = gather(lp0, up0)

    w0, w1 = call(
        pack123_kernel, [SMEM, SMEM, HBM, HBM],
        (sds(PACK, 128), sds(PACK, 128)), [pltpu.VMEM((NUM, 128), BF), dma((2,))], 56,
        ids0, role, left, upper,
    )
    w1 = send(w1, flip_leaf(1))
    m1, m2, m3, lp1, up1, own = call(
        deal_kernel, [SMEM, ANY, ANY],
        (
            sds(L2 + L3 + 2 * U + NUM, 128), sds(L3 + U + NUM, 128), sds(L3 + U + NUM, 128),
            sds(L1, 128), sds(U, 128), sds(L2 + L3 + 2 * U + NUM, 128),
        ),
        [dma((1,))], 8, role, w0, w1,
    )
    m1 = send(m1, flip_leaf(2))
    m2 = send(m2, flip_leaf(4))
    m3 = send(m3, flip_leaf(6))
    l1, u1 = gather(lp1, up1)

    t0 = call(
        update0_kernel, [SMEM, SMEM, VMEM] + [ANY] * 8, f32(front.shape[0]),
        [pltpu.VMEM((NODES, LIVE * BLK, inner), BF), pltpu.VMEM((NODES, inner, LIVE * BLK), BF), dma], 12,
        ids0, role, front, *l0, *u0,
    )
    r0 = send(t0, flip_leaf(1))

    z23, x23, nums = call(
        choose_kernel, [SMEM] + [ANY] * 4,
        (sds(L2 + L3, 128), sds(2 * U, 128), sds(3 * NUM, 128)), [dma], 4,
        role, own, m1, m2, m3,
    )
    per = NODES * SIDE * LIVE
    ids = jnp.stack([nums[j * NUM, j * per : (j + 1) * per] for j in range(3)]).astype(jnp.int32)
    ids = jnp.concatenate([ids0[:1], ids.reshape(3, NODES, SIDE * LIVE)])
    l23, u23 = gather(z23, x23)

    half = SLAB * 64
    keep, give = call(
        update1_kernel, [SMEM, SMEM, VMEM] + [ANY] * 8, (f32(half), f32(half)),
        panels(LIVE * BLK) + [pltpu.VMEM(front.shape, F32), dma], 12,
        ids, role, t0, *l1, *u1,
    )
    got = send(give, flip_leaf(1))
    keep, give = call(
        join_kernel, [SMEM, VMEM, VMEM], (f32(half // 2), codes(half // 2)),
        [pltpu.VMEM((half, cols), F32)], 8, role, keep, got,
    )
    got = send(give, flip_leaf(2))

    prods = f32(LIVE * 48, LIVE * BLK)
    mine, other = call(
        product23_kernel, [SMEM] + [ANY] * 8, (prods, prods),
        panels(LIVE * 64) + panels(LIVE * 32) + [dma((2,))], 8, role, *l23, *u23,
    )
    other = send(other, flip_leaf(1))

    s1, s1q, keep, give = call(
        update2_kernel, [SMEM, SMEM] + [VMEM] * 4,
        (f32(half // 2), codes(half // 2), f32(half // 4), codes(half // 4)),
        [pltpu.VMEM((half // 2, cols), F32)], 8, ids, role, keep, got, mine, other,
    )
    got = send(give, flip_leaf(4))
    piece = (f32(half // 4), codes(half // 4))
    s2, s2q, t3, t3q = call(
        update3_kernel, [SMEM, SMEM] + [VMEM] * 4, piece + piece, [], 8,
        ids, role, keep, got, mine, other,
    )
    r3 = send(t3q, flip_leaf(8))

    r1 = send(s1q, flip_leaf(2))
    e2 = []
    for j in (1, 2, 3):
        e2.append(send(s2q, flip_leaf(2 * j)))
    c12 = call(collect_kernel, [SMEM] + [ANY] * 6, codes(half), [dma], 4, role, s1q, r1, s2q, *e2)
    c12 = send(c12, flip_leaf(1))

    f8, f8q = call(last_kernel, [VMEM, VMEM], piece, [], 8, t3, r3)
    e3 = []
    for j in (1, 2, 3):
        e3.append(send(f8q, flip_leaf(2 * j)))
    c3 = [send(q, flip_leaf(1)) for q in [f8q] + e3]

    out = call(
        finish_kernel, [SMEM] + [ANY] * 17, f32(front.shape[0]),
        [
            pltpu.VMEM(front.shape, F32), pltpu.VMEM(front.shape, F32),
            pltpu.VMEM((7 * half // 4, cols + 128), jnp.int16), dma((3,)),
        ],
        8, role, t0, r0, s1, r1, s2, *e2, c12, f8, *e3, *c3, out_spec=ANY,
    )
    return out[None]


def solution(mesh):
    in_specs = (
        P("leaf", "row", "col"),
        P(None, None, "leaf", "row", "col"),
        P(None, None, "leaf", "row", "col"),
        P(None, None, "leaf", None),
    )
    out_specs = P("leaf", "row", "col")
    return jax.shard_map(on_device, mesh=mesh, in_specs=in_specs, out_specs=out_specs, check_vma=False)
```

time: 588 us -> 167 us (0.28)
  waiting for transfers between devices: 530 us -> 83.1 us
  starting transfers between devices: 6.53 us -> 50.1 us
  Pallas kernels: 0 us -> 25.6 us
  matrix products: 24.7 us -> 0 us
  between operations: 13.7 us -> 0.42 us
  other arithmetic: 7.24 us -> 1.29 us
    all_gather x8 -> x0, waiting for transfers between devices: 422 us -> none  [the longest x4 290 us: on_device(): left_all = lax.all_gather(left_rows, 'col', axis=2, tiled=True)]
    ppermute x4 -> x40, starting transfers between devices: 6.25 us -> 50.1 us  [send(): return lax.ppermute(x, AXES, pairs)]
    pallas_call x0 -> x13, Pallas kernels: none -> 25.6 us  [call(): pl.pallas_call(kernel, out_shape=outs, in_specs=specs, out_specs=jax.tree...]
    dot_general x4 -> x0, matrix products: 24.7 us -> none  [on_device(): lax.dot_general(left_all * row_mask[:, :, None], upper_all * col_mask[:,...]
    ppermute x4 -> x40, waiting for transfers between devices: 106 us -> 83.1 us  [send(): return lax.ppermute(x, AXES, pairs)]
  transfers between devices with their start and end apart: 12 -> 40, of which waited for: 9 -> 19; matrix products, arithmetic and copies ran while one was open for 5% -> 2% of each run, Pallas kernels for 0% -> 8%
where the time goes in v1:
time: 167 us; the launch traced here: 165 us
  waiting for transfers between devices  83.1 us (50%)
  starting transfers between devices  50.1 us (30%)
  Pallas kernels  25.6 us (15%)
  local copies, waits for them, and re-layouts  4.68 us (3%)
    ppermute x40, waiting for transfers between devices, send(): return lax.ppermute(x, AXES, pairs)  83.1 us
    ppermute x40, starting transfers between devices, send(): return lax.ppermute(x, AXES, pairs)  50.1 us
    pallas_call x13, Pallas kernels, call(): pl.pallas_call(kernel, out_shape=outs, in_specs=specs, out_specs=jax.tree...  25.6 us
  transfers between devices with their start and end apart: 40, of which 19 were waited for; matrix products, arithmetic and copies ran while one was open for 2% of the time, Pallas kernels for 8%

profile of v1, /device:TPU:3, one launch (start us, length us, event | category | flops | bytes accessed | tf_op | source)
XLA Modules:
  0.0 165.3 jit_solution(17300255322101229189)
XLA Ops:
  0.6 2.8 %shard_map.46 = (bf16[2,2,384,128]{3,2,1,0:T(8,128)(2,1)}, bf16[2,3,256,128]{3,2,1,0:T(8,128)(2,1)}) custom-call(s32[4,2,12]{2,1,0:T(2,128)} %bitcast.19, s32[4]{0:T(128)} %pad_add_fusion.1.role, bf16[4,2,1,768,256]{4,3,2,1,0:T(8,128)(2,1)} %left.2, bf16[4,2,1,256,768]{4,3,2,1,0:T(8,128)(2,1)} %upper.2), custom_call_target="tpu_custom_call" | custom-call | flops 1073741824 | bytes 4194304 | tf_op jit(solution)/shard_map/pallas_call | solution.py:366
  3.5 4.5 %shard_map.48 = (bf16[4624,128]{1,0:T(8,128)(2,1)}, bf16[4624,128]{1,0:T(8,128)(2,1)}) custom-call(s32[4,2,12]{2,1,0:T(2,128)} %bitcast.20, s32[4]{0:T(128)} %pad_add_fusion.1.role, bf16[4,2,1,768,256]{4,3,2,1,0:T(8,128)(2,1)} %left.2, bf16[4,2,1,256,768]{4,3,2,1,0:T(8,128)(2,1)} %upper.2), custom_call_target="tpu_custom_call" | custom-call | flops 1073741824 | bytes 4194304 | tf_op jit(solution)/shard_map/pallas_call | solution.py:366
  8.7 4.3 %collective-permute-start.2 = (bf16[1536,128]{1,0:T(8,128)(2,1)S(1)}, bf16[1536,128]{1,0:T(8,128)(2,1)S(1)}, u32[]{:S(2)}, u32[]{:S(2)}) collective-permute-start(bf16[1536,128]{1,0:T(8,128)(2,1)S(1)} %bitcast.11), channel_id=1, source_target_pairs={{0,48},{1,49},{2,50},{3,51},{4,52},{5,53},{6,54},{7,55},{8,56},{9,... | collective-permute-start | bytes 1179656 | tf_op jit(solution)/shard_map/ppermute | solution.py:45
  13.4 1.2 collective-permute-start.5
  14.6 1.3 copy-done.5
  15.9 3.1 %shard_map.49 = (bf16[2128,128]{1,0:T(8,128)(2,1)S(1)}, bf16[976,128]{1,0:T(8,128)(2,1)S(1)}, bf16[976,128]{1,0:T(8,128)(2,1)S(1)}, bf16[768,128]{1,0:T(8,128)(2...) custom-call(s32[4]{0:T(128)S(1)} %copy-done.4, bf16[4624,128]{1,0:T(8,128)(2,1)S(1)} %copy-done.5, ...), custom_call_target="tpu_custom_call" | custom-call | flops 1073741824 | bytes 4194304 | tf_op jit(solution)/shard_map/pallas_call | solution.py:366
  19.0 1.4 collective-permute-start.8
  20.4 2.2 %collective-permute-done.2.refs_3_ = bf16[1536,128]{1,0:T(8,128)(2,1)S(1)} collective-permute-done((bf16[1536,128]{1,0:T(8,128)(2,1)S(1)}, bf16[1536,128]{1,0:T(8,128)(2,1)S(1)}, u32[]{:S(2)}, u32[]{:S(2)}) %collective-permute-start.2) | collective-permute-done | bytes 393248 | tf_op jit(solution)/shard_map/ppermute | solution.py:45
  23.2 9.6 %collective-permute-done.1.refs_2_ = bf16[1536,128]{1,0:T(8,128)(2,1)S(1)} collective-permute-done((bf16[1536,128]{1,0:T(8,128)(2,1)S(1)}, bf16[1536,128]{1,0:T(8,128)(2,1)S(1)}, u32[]{:S(2)}, u32[]{:S(2)}) %collective-permute-start.1) | collective-permute-done | bytes 393248 | tf_op jit(solution)/shard_map/ppermute | solution.py:45
  32.7 1.8 %collective-permute-start.3 = (bf16[1536,128]{1,0:T(8,128)(2,1)S(1)}, bf16[1536,128]{1,0:T(8,128)(2,1)S(1)}, u32[]{:S(2)}, u32[]{:S(2)}) collective-permute-start(bf16[1536,128]{1,0:T(8,128)(2,1)S(1)} %bitcast.17), channel_id=1, source_target_pairs={{0,128},{1,129},{2,130},{3,131},{4,132},{5,133},{6,134},{7,135},{8... | collective-permute-start | bytes 1179656 | tf_op jit(solution)/shard_map/ppermute | solution.py:45
  34.6 11.7 %collective-permute-done.refs_1_ = bf16[1536,128]{1,0:T(8,128)(2,1)S(1)} collective-permute-done((bf16[1536,128]{1,0:T(8,128)(2,1)S(1)}, bf16[1536,128]{1,0:T(8,128)(2,1)S(1)}, u32[]{:S(2)}, u32[]{:S(2)}) %collective-permute-start) | collective-permute-done | bytes 393248 | tf_op jit(solution)/shard_map/ppermute | solution.py:45
  46.3 2.9 %collective-permute-start.9 = (bf16[976,128]{1,0:T(8,128)(2,1)S(1)}, bf16[976,128]{1,0:T(8,128)(2,1)S(1)}, u32[]{:S(2)}, u32[]{:S(2)}) collective-permute-start(bf16[976,128]{1,0:T(8,128)(2,1)S(1)} %get-tuple-element.48), channel_id=1, source_target_pairs={{0,4},{1,5},{2,6},{3,7},{4,0},{5,1},{6,2},{7,3},{8,12},{9,13},{10,... | collective-permute-start | bytes 749576 | tf_op jit(solution)/shard_map/ppermute | solution.py:45
  50.0 2.5 %shard_map.47.t0 = f32[768,768]{1,0:T(8,128)S(1)} custom-call(s32[4,2,12]{2,1,0:T(2,128)S(1)} %bitcast.21, s32[4]{0:T(128)S(1)} %copy-done.4, f32[768,768]{1,0:T(8,128)S(1)} %bitcast.10, bf16[1536,128]{1,0:T(8,128)(2,1)S(1)} %bitcast.14, bf16[1536,128]{1,0:T(8,128)(2,1)S(1)} %collective-permute-done.refs_1_, ...), custom_call_target="tpu_custom_call" | custom-call | flops 1073741824 | bytes 4194304 | tf_op jit(solution)/shard_map/pallas_call | solution.py:366
  52.5 2.3 %collective-permute-start.13 = (bf16[768,128]{1,0:T(8,128)(2,1)S(1)}, bf16[768,128]{1,0:T(8,128)(2,1)S(1)}, u32[]{:S(2)}, u32[]{:S(2)}) collective-permute-start(bf16[768,128]{1,0:T(8,128)(2,1)S(1)} %get-tuple-element.51.refs_0_), channel_id=1, source_target_pairs={{0,48},{1,49},{2,50},{3,51},{4,52},{5,53},{6,54},{7,55},{8,56},{9,... | collective-permute-start | bytes 589832 | tf_op jit(solution)/shard_map/ppermute | solution.py:45
  54.9 1.3 collective-permute-start.11
  56.2 4.9 %collective-permute-done.10.m3 = bf16[976,128]{1,0:T(8,128)(2,1)S(1)} collective-permute-done((bf16[976,128]{1,0:T(8,128)(2,1)S(1)}, bf16[976,128]{1,0:T(8,128)(2,1)S(1)}, u32[]{:S(2)}, u32[]{:S(2)}) %collective-permute-start.10) | collective-permute-done | bytes 249888 | tf_op jit(solution)/shard_map/ppermute | solution.py:45
  61.1 1.2 collective-permute-start.16
  62.3 1.5 collective-permute-start.15
  63.8 1.3 shard_map.50
  67.3 1.3 stack.30
  69.3 6.2 %collective-permute-done.14.refs_5_ = bf16[768,128]{1,0:T(8,128)(2,1)S(1)} collective-permute-done((bf16[768,128]{1,0:T(8,128)(2,1)S(1)}, bf16[768,128]{1,0:T(8,128)(2,1)S(1)}, u32[]{:S(2)}, u32[]{:S(2)}) %collective-permute-start.14) | collective-permute-done | bytes 196640 | tf_op jit(solution)/shard_map/ppermute | solution.py:45
  75.4 2.6 %shard_map.51 = (f32[384,768]{1,0:T(8,128)S(1)}, f32[384,768]{1,0:T(8,128)S(1)}) custom-call(s32[4,2,12]{2,1,0:T(2,128)S(1)} %pad_add_fusion.ids, s32[4]{0:T(128)S(1)} %copy-done.4, f32[768,768]{1,0:T(8,128)S(1)} %shard_map.47.t0, bf16[768,128]{1,0:T(8,128)(2,1)S(1)} %get-tuple-element.51.refs_0_, bf16[768,128]{1,0:T(8,128)(2,1)} %collective-permute-done.11.refs_1_, ...), custom_call_target="tpu_custom_call" | custom-call | flops 1073741824 | bytes 4194304 | tf_op jit(solution)/shard_map/pallas_call | solution.py:366
  78.0 2.0 %collective-permute-start.17 = (f32[384,768]{1,0:T(8,128)S(1)}, f32[384,768]{1,0:T(8,128)S(1)}, u32[]{:S(2)}, u32[]{:S(2)}) collective-permute-start(f32[384,768]{1,0:T(8,128)S(1)} %get-tuple-element.54), channel_id=1, source_target_pairs={{0,1},{1,0},{2,3},{3,2},{4,5},{5,4},{6,7},{7,6},{8,9},{9,8},{10,11... | collective-permute-start | bytes 3538952 | tf_op jit(solution)/shard_map/ppermute | solution.py:45
  80.1 2.2 %collective-permute-start.21 = (bf16[576,128]{1,0:T(8,128)(2,1)S(1)}, bf16[576,128]{1,0:T(8,128)(2,1)S(1)}, u32[]{:S(2)}, u32[]{:S(2)}) collective-permute-start(bf16[576,128]{1,0:T(8,128)(2,1)S(1)} %copy-done.7), channel_id=1, source_target_pairs={{0,48},{1,49},{2,50},{3,51},{4,52},{5,53},{6,54},{7,55},{8,56},{9,... | collective-permute-start | bytes 442376 | tf_op jit(solution)/shard_map/ppermute | solution.py:45
  82.4 4.6 %collective-permute-done.21.refs_3_ = bf16[576,128]{1,0:T(8,128)(2,1)S(1)} collective-permute-done((bf16[576,128]{1,0:T(8,128)(2,1)S(1)}, bf16[576,128]{1,0:T(8,128)(2,1)S(1)}, u32[]{:S(2)}, u32[]{:S(2)}) %collective-permute-start.21) | collective-permute-done | bytes 147488 | tf_op jit(solution)/shard_map/ppermute | solution.py:45
  87.0 4.0 %collective-permute-done.20.refs_2_ = bf16[576,128]{1,0:T(8,128)(2,1)S(1)} collective-permute-done((bf16[576,128]{1,0:T(8,128)(2,1)S(1)}, bf16[576,128]{1,0:T(8,128)(2,1)S(1)}, u32[]{:S(2)}, u32[]{:S(2)}) %collective-permute-start.20) | collective-permute-done | bytes 147488 | tf_op jit(solution)/shard_map/ppermute | solution.py:45
  92.0 7.8 %collective-permute-done.19.refs_1_ = bf16[576,128]{1,0:T(8,128)(2,1)S(1)} collective-permute-done((bf16[576,128]{1,0:T(8,128)(2,1)S(1)}, bf16[576,128]{1,0:T(8,128)(2,1)S(1)}, u32[]{:S(2)}, u32[]{:S(2)}) %collective-permute-start.19) | collective-permute-done | bytes 147488 | tf_op jit(solution)/shard_map/ppermute | solution.py:45
  99.8 1.3 collective-permute-start.18
  101.1 2.5 %collective-permute-done.22.refs_5_ = bf16[1536,128]{1,0:T(8,128)(2,1)S(1)} collective-permute-done((bf16[1536,128]{1,0:T(8,128)(2,1)S(1)}, bf16[1536,128]{1,0:T(8,128)(2,1)S(1)}, u32[]{:S(2)}, u32[]{:S(2)}) %collective-permute-start.22) | collective-permute-done | bytes 393248 | tf_op jit(solution)/shard_map/ppermute | solution.py:45
  103.6 1.7 %shard_map.53 = (f32[144,384]{1,0:T(8,128)S(1)}, f32[144,384]{1,0:T(8,128)S(1)}) custom-call(s32[4]{0:T(128)S(1)} %copy-done.4, bf16[576,128]{1,0:T(8,128)(2,1)S(1)} %copy-done.7, bf16[576,128]{1,0:T(8,128)(2,1)S(1)} %collective-permute-done.19.refs_1_, bf16[576,128]{1,0:T(8,128)(2,1)S(1)} %collective-permute-done.20.refs_2_, ...), custom_call_target="tpu_custom_call" | custom-call | flops 1073741824 | bytes 4194304 | tf_op jit(solution)/shard_map/pallas_call | solution.py:366
  105.3 2.8 %collective-permute-start.25 = (f32[144,384]{1,0:T(8,128)S(1)}, f32[144,384]{1,0:T(8,128)S(1)}, u32[]{:S(2)}, u32[]{:S(2)}) collective-permute-start(f32[144,384]{1,0:T(8,128)S(1)} %get-tuple-element.60), channel_id=1, source_target_pairs={{0,1},{1,0},{2,3},{3,2},{4,5},{5,4},{6,7},{7,6},{8,9},{9,8},{10,11... | collective-permute-start | bytes 663560 | tf_op jit(solution)/shard_map/ppermute | solution.py:45
  108.1 1.1 collective-permute-done.25.theirs
  109.2 1.1 shard_map.54
  110.3 2.3 %collective-permute-start.27 = (s16[96,896]{1,0:T(8,128)(2,1)S(1)}, s16[96,896]{1,0:T(8,128)(2,1)S(1)}, u32[]{:S(2)}, u32[]{:S(2)}) collective-permute-start(s16[96,896]{1,0:T(8,128)(2,1)S(1)} %get-tuple-element.64), channel_id=1, source_target_pairs={{0,4},{1,5},{2,6},{3,7},{4,0},{5,1},{6,2},{7,3},{8,12},{9,13},{10,... | collective-permute-start | bytes 516104 | tf_op jit(solution)/shard_map/ppermute | solution.py:45
  113.6 3.1 %collective-permute-done.27.b = s16[96,896]{1,0:T(8,128)(2,1)S(1)} collective-permute-done((s16[96,896]{1,0:T(8,128)(2,1)S(1)}, s16[96,896]{1,0:T(8,128)(2,1)S(1)}, u32[]{:S(2)}, u32[]{:S(2)}) %collective-permute-start.27) | collective-permute-done | bytes 172064 | tf_op jit(solution)/shard_map/ppermute | solution.py:45
  117.6 2.7 %collective-permute-start.30 = (s16[96,896]{1,0:T(8,128)(2,1)S(1)}, s16[96,896]{1,0:T(8,128)(2,1)S(1)}, u32[]{:S(2)}, u32[]{:S(2)}) collective-permute-start(s16[96,896]{1,0:T(8,128)(2,1)S(1)} %get-tuple-element.66.s2), channel_id=1, source_target_pairs={{0,6},{1,7},{2,4},{3,5},{4,2},{5,3},{6,0},{7,1},{8,14},{9,15},{10,... | collective-permute-start | bytes 516104 | tf_op jit(solution)/shard_map/ppermute | solution.py:45
  121.0 2.1 %collective-permute-done.30.refs_2_ = s16[96,896]{1,0:T(8,128)(2,1)S(1)} collective-permute-done((s16[96,896]{1,0:T(8,128)(2,1)S(1)}, s16[96,896]{1,0:T(8,128)(2,1)S(1)}, u32[]{:S(2)}, u32[]{:S(2)}) %collective-permute-start.30) | collective-permute-done | bytes 172064 | tf_op jit(solution)/shard_map/ppermute | solution.py:45
  123.2 4.1 %collective-permute-done.29.refs_1_ = s16[96,896]{1,0:T(8,128)(2,1)S(1)} collective-permute-done((s16[96,896]{1,0:T(8,128)(2,1)S(1)}, s16[96,896]{1,0:T(8,128)(2,1)S(1)}, u32[]{:S(2)}, u32[]{:S(2)}) %collective-permute-start.29) | collective-permute-done | bytes 172064 | tf_op jit(solution)/shard_map/ppermute | solution.py:45
  127.3 4.4 %collective-permute-done.28.refs_0_ = s16[96,896]{1,0:T(8,128)(2,1)S(1)} collective-permute-done((s16[96,896]{1,0:T(8,128)(2,1)S(1)}, s16[96,896]{1,0:T(8,128)(2,1)S(1)}, u32[]{:S(2)}, u32[]{:S(2)}) %collective-permute-start.28) | collective-permute-done | bytes 172064 | tf_op jit(solution)/shard_map/ppermute | solution.py:45
  131.7 1.5 shard_map.56
  133.2 2.1 %collective-permute-start.31 = (s16[384,896]{1,0:T(8,128)(2,1)S(1)}, s16[384,896]{1,0:T(8,128)(2,1)S(1)}, u32[]{:S(2)}, u32[]{:S(2)}) collective-permute-start(s16[384,896]{1,0:T(8,128)(2,1)S(1)} %shard_map.56), channel_id=1, source_target_pairs={{0,1},{1,0},{2,3},{3,2},{4,5},{5,4},{6,7},{7,6},{8,9},{9,8},{10,11... | collective-permute-start | bytes 2064392 | tf_op jit(solution)/shard_map/ppermute | solution.py:45
  135.3 5.7 %collective-permute-start.32 = (s16[96,896]{1,0:T(8,128)(2,1)S(1)}, s16[96,896]{1,0:T(8,128)(2,1)S(1)}, u32[]{:S(2)}, u32[]{:S(2)}) collective-permute-start(s16[96,896]{1,0:T(8,128)(2,1)S(1)} %get-tuple-element.68), channel_id=1, source_target_pairs={{0,8},{1,9},{2,10},{3,11},{4,12},{5,13},{6,14},{7,15},{8,0},{9,1},... | collective-permute-start | bytes 516104 | tf_op jit(solution)/shard_map/ppermute | solution.py:45
  140.9 8.0 %collective-permute-done.32.r = s16[96,896]{1,0:T(8,128)(2,1)S(1)} collective-permute-done((s16[96,896]{1,0:T(8,128)(2,1)S(1)}, s16[96,896]{1,0:T(8,128)(2,1)S(1)}, u32[]{:S(2)}, u32[]{:S(2)}) %collective-permute-start.32) | collective-permute-done | bytes 172064 | tf_op jit(solution)/shard_map/ppermute | solution.py:45
  149.2 1.7 collective-permute-start.34
  150.9 1.6 collective-permute-start.33
  152.5 1.9 %collective-permute-start.36 = (s16[96,896]{1,0:T(8,128)(2,1)S(1)}, s16[96,896]{1,0:T(8,128)(2,1)S(1)}, u32[]{:S(2)}, u32[]{:S(2)}) collective-permute-start(s16[96,896]{1,0:T(8,128)(2,1)S(1)} %get-tuple-element.70), channel_id=1, source_target_pairs={{0,1},{1,0},{2,3},{3,2},{4,5},{5,4},{6,7},{7,6},{8,9},{9,8},{10,11... | collective-permute-start | bytes 516104 | tf_op jit(solution)/shard_map/ppermute | solution.py:45
  154.3 5.7 %collective-permute-done.35.refs_7_ = s16[96,896]{1,0:T(8,128)(2,1)S(1)} collective-permute-done((s16[96,896]{1,0:T(8,128)(2,1)S(1)}, s16[96,896]{1,0:T(8,128)(2,1)S(1)}, u32[]{:S(2)}, u32[]{:S(2)}) %collective-permute-start.35) | collective-permute-done | bytes 172064 | tf_op jit(solution)/shard_map/ppermute | solution.py:45
  162.6 2.5 %shard_map.58 = f32[768,768]{1,0:T(8,128)} custom-call(s32[4]{0:T(128)S(1)} %copy-done.4, f32[768,768]{1,0:T(8,128)S(1)} %shard_map.47.t0, f32[768,768]{1,0:T(8,128)S(1)} %collective-permute-done.6.r0, f32[192,768]{1,0:T(8,128)S(1)} %get-tuple-element.61.s1, s16[192,896]{1,0:T(8,128)(2,1)S(1)} %collective-permute-done.26.r1, ...), custom_call_target="tpu_custom_call" | custom-call | flops 1073741824 | bytes 4194304 | tf_op jit(solution)/shard_map/pallas_call | solution.py:366
  (69 shorter events, 12.5 us)
Async XLA Ops:
  3.5 5.3 %copy-start.1 = (bf16[2,2,384,128]{3,2,1,0:T(8,128)(2,1)S(1)}, bf16[2,2,384,128]{3,2,1,0:T(8,128)(2,1)}, u32[]{:S(2)}) copy-start(bf16[2,2,384,128]{3,2,1,0:T(8,128)(2,1)} %get-tuple-element.38) | copy-start | bytes 1179652
  3.5 9.9 %copy-start.2 = (bf16[2,3,256,128]{3,2,1,0:T(8,128)(2,1)S(1)}, bf16[2,3,256,128]{3,2,1,0:T(8,128)(2,1)}, u32[]{:S(2)}) copy-start(bf16[2,3,256,128]{3,2,1,0:T(8,128)(2,1)} %get-tuple-element.39) | copy-start | bytes 1179652
  3.5 11.1 %copy-start.4 = (s32[4]{0:T(128)S(1)}, s32[4]{0:T(128)}, u32[]{:S(2)}) copy-start(s32[4]{0:T(128)} %pad_add_fusion.1.role) | copy-start | bytes 52
  7.9 42.0 %copy-start.3 = (s32[4,2,1,12]{3,2,1,0:T(1,128)S(1)}, s32[4,2,1,12]{3,2,1,0:T(1,128)}, u32[]{:S(2)}) copy-start(s32[4,2,1,12]{3,2,1,0:T(1,128)} %param.7) | copy-start | bytes 1156
  8.0 42.0 %copy-start = (f32[1,768,768]{2,1,0:T(8,128)S(1)}, f32[1,768,768]{2,1,0:T(8,128)}, u32[]{:S(2)}) copy-start(f32[1,768,768]{2,1,0:T(8,128)} %param.4) | copy-start | bytes 7077892
  8.0 6.6 %collective-permute-start.7 = (bf16[4624,128]{1,0:T(8,128)(2,1)}, bf16[4624,128]{1,0:T(8,128)(2,1)S(1)}, u32[]{:S(2)}, u32[]{:S(2)}) collective-permute-start(bf16[4624,128]{1,0:T(8,128)(2,1)} %get-tuple-element.45), channel_id=1, source_target_pairs={{0,1},{1,0},{2,3},{3,2},{4,5},{5,4},{6,7},{7,6},{8,9},{9,8},{10,11... | collective-permute-start | bytes 3551240 | tf_op jit(solution)/shard_map/ppermute | solution.py:45
  8.7 13.8 %collective-permute-start.2 = (bf16[1536,128]{1,0:T(8,128)(2,1)S(1)}, bf16[1536,128]{1,0:T(8,128)(2,1)S(1)}, u32[]{:S(2)}, u32[]{:S(2)}) collective-permute-start(bf16[1536,128]{1,0:T(8,128)(2,1)S(1)} %bitcast.11), channel_id=1, source_target_pairs={{0,48},{1,49},{2,50},{3,51},{4,52},{5,53},{6,54},{7,55},{8,56},{9,... | collective-permute-start | bytes 1179656 | tf_op jit(solution)/shard_map/ppermute | solution.py:45
  13.1 19.7 %collective-permute-start.1 = (bf16[1536,128]{1,0:T(8,128)(2,1)S(1)}, bf16[1536,128]{1,0:T(8,128)(2,1)S(1)}, u32[]{:S(2)}, u32[]{:S(2)}) collective-permute-start(bf16[1536,128]{1,0:T(8,128)(2,1)S(1)} %bitcast.12), channel_id=1, source_target_pairs={{0,16},{1,17},{2,18},{3,19},{4,20},{5,21},{6,22},{7,23},{8,24},{9,... | collective-permute-start | bytes 1179656 | tf_op jit(solution)/shard_map/ppermute | solution.py:45
  13.1 33.2 %collective-permute-start = (bf16[1536,128]{1,0:T(8,128)(2,1)S(1)}, bf16[1536,128]{1,0:T(8,128)(2,1)S(1)}, u32[]{:S(2)}, u32[]{:S(2)}) collective-permute-start(bf16[1536,128]{1,0:T(8,128)(2,1)S(1)} %bitcast.13), channel_id=1, source_target_pairs={{0,32},{1,33},{2,34},{3,35},{4,36},{5,37},{6,38},{7,39},{8,40},{9,... | collective-permute-start | bytes 1179656 | tf_op jit(solution)/shard_map/ppermute | solution.py:45
  13.4 35.8 %collective-permute-start.5 = (bf16[1536,128]{1,0:T(8,128)(2,1)S(1)}, bf16[1536,128]{1,0:T(8,128)(2,1)S(1)}, u32[]{:S(2)}, u32[]{:S(2)}) collective-permute-start(bf16[1536,128]{1,0:T(8,128)(2,1)S(1)} %bitcast.15), channel_id=1, source_target_pairs={{0,192},{1,193},{2,194},{3,195},{4,196},{5,197},{6,198},{7,199},{8... | collective-permute-start | bytes 1179656 | tf_op jit(solution)/shard_map/ppermute | solution.py:45
  14.6 1.3 copy-start.5
  19.0 43.3 %collective-permute-start.8 = (bf16[2128,128]{1,0:T(8,128)(2,1)S(1)}, bf16[2128,128]{1,0:T(8,128)(2,1)S(1)}, u32[]{:S(2)}, u32[]{:S(2)}) collective-permute-start(bf16[2128,128]{1,0:T(8,128)(2,1)S(1)} %get-tuple-element.47), channel_id=1, source_target_pairs={{0,2},{1,3},{2,0},{3,1},{4,6},{5,7},{6,4},{7,5},{8,10},{9,11},{10,... | collective-permute-start | bytes 1634312 | tf_op jit(solution)/shard_map/ppermute | solution.py:45
  22.5 27.4 %collective-permute-start.4 = (bf16[1536,128]{1,0:T(8,128)(2,1)S(1)}, bf16[1536,128]{1,0:T(8,128)(2,1)S(1)}, u32[]{:S(2)}, u32[]{:S(2)}) collective-permute-start(bf16[1536,128]{1,0:T(8,128)(2,1)S(1)} %bitcast.16), channel_id=1, source_target_pairs={{0,64},{1,65},{2,66},{3,67},{4,68},{5,69},{6,70},{7,71},{8,72},{9,... | collective-permute-start | bytes 1179656 | tf_op jit(solution)/shard_map/ppermute | solution.py:45
  32.7 17.2 %collective-permute-start.3 = (bf16[1536,128]{1,0:T(8,128)(2,1)S(1)}, bf16[1536,128]{1,0:T(8,128)(2,1)S(1)}, u32[]{:S(2)}, u32[]{:S(2)}) collective-permute-start(bf16[1536,128]{1,0:T(8,128)(2,1)S(1)} %bitcast.17), channel_id=1, source_target_pairs={{0,128},{1,129},{2,130},{3,131},{4,132},{5,133},{6,134},{7,135},{8... | collective-permute-start | bytes 1179656 | tf_op jit(solution)/shard_map/ppermute | solution.py:45
  46.3 8.6 %collective-permute-start.9 = (bf16[976,128]{1,0:T(8,128)(2,1)S(1)}, bf16[976,128]{1,0:T(8,128)(2,1)S(1)}, u32[]{:S(2)}, u32[]{:S(2)}) collective-permute-start(bf16[976,128]{1,0:T(8,128)(2,1)S(1)} %get-tuple-element.48), channel_id=1, source_target_pairs={{0,4},{1,5},{2,6},{3,7},{4,0},{5,1},{6,2},{7,3},{8,12},{9,13},{10,... | collective-permute-start | bytes 749576 | tf_op jit(solution)/shard_map/ppermute | solution.py:45
  49.2 11.9 %collective-permute-start.10 = (bf16[976,128]{1,0:T(8,128)(2,1)S(1)}, bf16[976,128]{1,0:T(8,128)(2,1)S(1)}, u32[]{:S(2)}, u32[]{:S(2)}) collective-permute-start(bf16[976,128]{1,0:T(8,128)(2,1)S(1)} %get-tuple-element.49), channel_id=1, source_target_pairs={{0,6},{1,7},{2,4},{3,5},{4,2},{5,3},{6,0},{7,1},{8,14},{9,15},{10,... | collective-permute-start | bytes 749576 | tf_op jit(solution)/shard_map/ppermute | solution.py:45
  52.5 16.0 %collective-permute-start.13 = (bf16[768,128]{1,0:T(8,128)(2,1)S(1)}, bf16[768,128]{1,0:T(8,128)(2,1)S(1)}, u32[]{:S(2)}, u32[]{:S(2)}) collective-permute-start(bf16[768,128]{1,0:T(8,128)(2,1)S(1)} %get-tuple-element.51.refs_0_), channel_id=1, source_target_pairs={{0,48},{1,49},{2,50},{3,51},{4,52},{5,53},{6,54},{7,55},{8,56},{9,... | collective-permute-start | bytes 589832 | tf_op jit(solution)/shard_map/ppermute | solution.py:45
  54.9 14.4 %collective-permute-start.12 = (bf16[768,128]{1,0:T(8,128)(2,1)S(1)}, bf16[768,128]{1,0:T(8,128)(2,1)S(1)}, u32[]{:S(2)}, u32[]{:S(2)}) collective-permute-start(bf16[768,128]{1,0:T(8,128)(2,1)S(1)} %get-tuple-element.51.refs_0_), channel_id=1, source_target_pairs={{0,16},{1,17},{2,18},{3,19},{4,20},{5,21},{6,22},{7,23},{8,24},{9,... | collective-permute-start | bytes 589832 | tf_op jit(solution)/shard_map/ppermute | solution.py:45
  54.9 14.4 %collective-permute-start.11 = (bf16[768,128]{1,0:T(8,128)(2,1)S(1)}, bf16[768,128]{1,0:T(8,128)(2,1)}, u32[]{:S(2)}, u32[]{:S(2)}) collective-permute-start(bf16[768,128]{1,0:T(8,128)(2,1)S(1)} %get-tuple-element.51.refs_0_), channel_id=1, source_target_pairs={{0,32},{1,33},{2,34},{3,35},{4,36},{5,37},{6,38},{7,39},{8,40},{9,... | collective-permute-start | bytes 589832 | tf_op jit(solution)/shard_map/ppermute | solution.py:45
  61.1 8.1 %collective-permute-start.16 = (bf16[768,128]{1,0:T(8,128)(2,1)S(1)}, bf16[768,128]{1,0:T(8,128)(2,1)}, u32[]{:S(2)}, u32[]{:S(2)}) collective-permute-start(bf16[768,128]{1,0:T(8,128)(2,1)S(1)} %get-tuple-element.52.refs_4_), channel_id=1, source_target_pairs={{0,192},{1,193},{2,194},{3,195},{4,196},{5,197},{6,198},{7,199},{8... | collective-permute-start | bytes 589832 | tf_op jit(solution)/shard_map/ppermute | solution.py:45
  62.3 6.9 %collective-permute-start.15 = (bf16[768,128]{1,0:T(8,128)(2,1)S(1)}, bf16[768,128]{1,0:T(8,128)(2,1)}, u32[]{:S(2)}, u32[]{:S(2)}) collective-permute-start(bf16[768,128]{1,0:T(8,128)(2,1)S(1)} %get-tuple-element.52.refs_4_), channel_id=1, source_target_pairs={{0,64},{1,65},{2,66},{3,67},{4,68},{5,69},{6,70},{7,71},{8,72},{9,... | collective-permute-start | bytes 589832 | tf_op jit(solution)/shard_map/ppermute | solution.py:45
  65.1 0.7 copy-start.6
  68.5 11.6 %copy-start.7 = (bf16[576,128]{1,0:T(8,128)(2,1)S(1)}, bf16[576,128]{1,0:T(8,128)(2,1)}, u32[]{:S(2)}) copy-start(bf16[576,128]{1,0:T(8,128)(2,1)} %copy-done.6) | copy-start | bytes 442372
  68.5 6.9 %collective-permute-start.14 = (bf16[768,128]{1,0:T(8,128)(2,1)S(1)}, bf16[768,128]{1,0:T(8,128)(2,1)S(1)}, u32[]{:S(2)}, u32[]{:S(2)}) collective-permute-start(bf16[768,128]{1,0:T(8,128)(2,1)S(1)} %get-tuple-element.52.refs_4_), channel_id=1, source_target_pairs={{0,128},{1,129},{2,130},{3,131},{4,132},{5,133},{6,134},{7,135},{8... | collective-permute-start | bytes 589832 | tf_op jit(solution)/shard_map/ppermute | solution.py:45
  78.0 12.9 %collective-permute-start.17 = (f32[384,768]{1,0:T(8,128)S(1)}, f32[384,768]{1,0:T(8,128)S(1)}, u32[]{:S(2)}, u32[]{:S(2)}) collective-permute-start(f32[384,768]{1,0:T(8,128)S(1)} %get-tuple-element.54), channel_id=1, source_target_pairs={{0,1},{1,0},{2,3},{3,2},{4,5},{5,4},{6,7},{7,6},{8,9},{9,8},{10,11... | collective-permute-start | bytes 3538952 | tf_op jit(solution)/shard_map/ppermute | solution.py:45
  80.0 72.4 %collective-permute-start.6 = (f32[768,768]{1,0:T(8,128)S(1)}, f32[768,768]{1,0:T(8,128)S(1)}, u32[]{:S(2)}, u32[]{:S(2)}) collective-permute-start(f32[768,768]{1,0:T(8,128)S(1)} %shard_map.47.t0), channel_id=1, source_target_pairs={{0,1},{1,0},{2,3},{3,2},{4,5},{5,4},{6,7},{7,6},{8,9},{9,8},{10,11... | collective-permute-start | bytes 7077896 | tf_op jit(solution)/shard_map/ppermute | solution.py:45
  80.1 6.8 %collective-permute-start.21 = (bf16[576,128]{1,0:T(8,128)(2,1)S(1)}, bf16[576,128]{1,0:T(8,128)(2,1)S(1)}, u32[]{:S(2)}, u32[]{:S(2)}) collective-permute-start(bf16[576,128]{1,0:T(8,128)(2,1)S(1)} %copy-done.7), channel_id=1, source_target_pairs={{0,48},{1,49},{2,50},{3,51},{4,52},{5,53},{6,54},{7,55},{8,56},{9,... | collective-permute-start | bytes 442376 | tf_op jit(solution)/shard_map/ppermute | solution.py:45
  82.4 8.6 %collective-permute-start.20 = (bf16[576,128]{1,0:T(8,128)(2,1)S(1)}, bf16[576,128]{1,0:T(8,128)(2,1)S(1)}, u32[]{:S(2)}, u32[]{:S(2)}) collective-permute-start(bf16[576,128]{1,0:T(8,128)(2,1)S(1)} %copy-done.7), channel_id=1, source_target_pairs={{0,16},{1,17},{2,18},{3,19},{4,20},{5,21},{6,22},{7,23},{8,24},{9,... | collective-permute-start | bytes 442376 | tf_op jit(solution)/shard_map/ppermute | solution.py:45
  82.4 18.7 %collective-permute-start.24 = (bf16[1536,128]{1,0:T(8,128)(2,1)S(1)}, bf16[1536,128]{1,0:T(8,128)(2,1)S(1)}, u32[]{:S(2)}, u32[]{:S(2)}) collective-permute-start(bf16[1536,128]{1,0:T(8,128)(2,1)S(1)} %get-tuple-element.58.refs_4_), channel_id=1, source_target_pairs={{0,192},{1,193},{2,194},{3,195},{4,196},{5,197},{6,198},{7,199},{8... | collective-permute-start | bytes 1179656 | tf_op jit(solution)/shard_map/ppermute | solution.py:45
  87.0 14.1 %collective-permute-start.23 = (bf16[1536,128]{1,0:T(8,128)(2,1)S(1)}, bf16[1536,128]{1,0:T(8,128)(2,1)S(1)}, u32[]{:S(2)}, u32[]{:S(2)}) collective-permute-start(bf16[1536,128]{1,0:T(8,128)(2,1)S(1)} %get-tuple-element.58.refs_4_), channel_id=1, source_target_pairs={{0,64},{1,65},{2,66},{3,67},{4,68},{5,69},{6,70},{7,71},{8,72},{9,... | collective-permute-start | bytes 1179656 | tf_op jit(solution)/shard_map/ppermute | solution.py:45
  91.0 12.6 %collective-permute-start.22 = (bf16[1536,128]{1,0:T(8,128)(2,1)S(1)}, bf16[1536,128]{1,0:T(8,128)(2,1)S(1)}, u32[]{:S(2)}, u32[]{:S(2)}) collective-permute-start(bf16[1536,128]{1,0:T(8,128)(2,1)S(1)} %get-tuple-element.58.refs_4_), channel_id=1, source_target_pairs={{0,128},{1,129},{2,130},{3,131},{4,132},{5,133},{6,134},{7,135},{8... | collective-permute-start | bytes 1179656 | tf_op jit(solution)/shard_map/ppermute | solution.py:45
  91.0 8.8 %collective-permute-start.19 = (bf16[576,128]{1,0:T(8,128)(2,1)S(1)}, bf16[576,128]{1,0:T(8,128)(2,1)S(1)}, u32[]{:S(2)}, u32[]{:S(2)}) collective-permute-start(bf16[576,128]{1,0:T(8,128)(2,1)S(1)} %copy-done.7), channel_id=1, source_target_pairs={{0,32},{1,33},{2,34},{3,35},{4,36},{5,37},{6,38},{7,39},{8,40},{9,... | collective-permute-start | bytes 442376 | tf_op jit(solution)/shard_map/ppermute | solution.py:45
  99.8 9.4 %collective-permute-start.18 = (s16[192,896]{1,0:T(8,128)(2,1)S(1)}, s16[192,896]{1,0:T(8,128)(2,1)S(1)}, u32[]{:S(2)}, u32[]{:S(2)}) collective-permute-start(s16[192,896]{1,0:T(8,128)(2,1)S(1)} %get-tuple-element.56), channel_id=1, source_target_pairs={{0,2},{1,3},{2,0},{3,1},{4,6},{5,7},{6,4},{7,5},{8,10},{9,11},{10,... | collective-permute-start | bytes 1032200 | tf_op jit(solution)/shard_map/ppermute | solution.py:45
  105.3 3.9 %collective-permute-start.25 = (f32[144,384]{1,0:T(8,128)S(1)}, f32[144,384]{1,0:T(8,128)S(1)}, u32[]{:S(2)}, u32[]{:S(2)}) collective-permute-start(f32[144,384]{1,0:T(8,128)S(1)} %get-tuple-element.60), channel_id=1, source_target_pairs={{0,1},{1,0},{2,3},{3,2},{4,5},{5,4},{6,7},{7,6},{8,9},{9,8},{10,11... | collective-permute-start | bytes 663560 | tf_op jit(solution)/shard_map/ppermute | solution.py:45
  110.3 6.4 %collective-permute-start.27 = (s16[96,896]{1,0:T(8,128)(2,1)S(1)}, s16[96,896]{1,0:T(8,128)(2,1)S(1)}, u32[]{:S(2)}, u32[]{:S(2)}) collective-permute-start(s16[96,896]{1,0:T(8,128)(2,1)S(1)} %get-tuple-element.64), channel_id=1, source_target_pairs={{0,4},{1,5},{2,6},{3,7},{4,0},{5,1},{6,2},{7,3},{8,12},{9,13},{10,... | collective-permute-start | bytes 516104 | tf_op jit(solution)/shard_map/ppermute | solution.py:45
  112.6 19.1 %collective-permute-start.26 = (s16[192,896]{1,0:T(8,128)(2,1)S(1)}, s16[192,896]{1,0:T(8,128)(2,1)S(1)}, u32[]{:S(2)}, u32[]{:S(2)}) collective-permute-start(s16[192,896]{1,0:T(8,128)(2,1)S(1)} %get-tuple-element.62.s1), channel_id=1, source_target_pairs={{0,2},{1,3},{2,0},{3,1},{4,6},{5,7},{6,4},{7,5},{8,10},{9,11},{10,... | collective-permute-start | bytes 1032200 | tf_op jit(solution)/shard_map/ppermute | solution.py:45
  117.6 5.6 %collective-permute-start.30 = (s16[96,896]{1,0:T(8,128)(2,1)S(1)}, s16[96,896]{1,0:T(8,128)(2,1)S(1)}, u32[]{:S(2)}, u32[]{:S(2)}) collective-permute-start(s16[96,896]{1,0:T(8,128)(2,1)S(1)} %get-tuple-element.66.s2), channel_id=1, source_target_pairs={{0,6},{1,7},{2,4},{3,5},{4,2},{5,3},{6,0},{7,1},{8,14},{9,15},{10,... | collective-permute-start | bytes 516104 | tf_op jit(solution)/shard_map/ppermute | solution.py:45
  120.4 6.9 %collective-permute-start.29 = (s16[96,896]{1,0:T(8,128)(2,1)S(1)}, s16[96,896]{1,0:T(8,128)(2,1)S(1)}, u32[]{:S(2)}, u32[]{:S(2)}) collective-permute-start(s16[96,896]{1,0:T(8,128)(2,1)S(1)} %get-tuple-element.66.s2), channel_id=1, source_target_pairs={{0,4},{1,5},{2,6},{3,7},{4,0},{5,1},{6,2},{7,3},{8,12},{9,13},{10,... | collective-permute-start | bytes 516104 | tf_op jit(solution)/shard_map/ppermute | solution.py:45
  120.7 11.0 %collective-permute-start.28 = (s16[96,896]{1,0:T(8,128)(2,1)S(1)}, s16[96,896]{1,0:T(8,128)(2,1)S(1)}, u32[]{:S(2)}, u32[]{:S(2)}) collective-permute-start(s16[96,896]{1,0:T(8,128)(2,1)S(1)} %get-tuple-element.66.s2), channel_id=1, source_target_pairs={{0,2},{1,3},{2,0},{3,1},{4,6},{5,7},{6,4},{7,5},{8,10},{9,11},{10,... | collective-permute-start | bytes 516104 | tf_op jit(solution)/shard_map/ppermute | solution.py:45
  133.2 29.4 %collective-permute-start.31 = (s16[384,896]{1,0:T(8,128)(2,1)S(1)}, s16[384,896]{1,0:T(8,128)(2,1)S(1)}, u32[]{:S(2)}, u32[]{:S(2)}) collective-permute-start(s16[384,896]{1,0:T(8,128)(2,1)S(1)} %shard_map.56), channel_id=1, source_target_pairs={{0,1},{1,0},{2,3},{3,2},{4,5},{5,4},{6,7},{7,6},{8,9},{9,8},{10,11... | collective-permute-start | bytes 2064392 | tf_op jit(solution)/shard_map/ppermute | solution.py:45
  135.3 13.7 %collective-permute-start.32 = (s16[96,896]{1,0:T(8,128)(2,1)S(1)}, s16[96,896]{1,0:T(8,128)(2,1)S(1)}, u32[]{:S(2)}, u32[]{:S(2)}) collective-permute-start(s16[96,896]{1,0:T(8,128)(2,1)S(1)} %get-tuple-element.68), channel_id=1, source_target_pairs={{0,8},{1,9},{2,10},{3,11},{4,12},{5,13},{6,14},{7,15},{8,0},{9,1},... | collective-permute-start | bytes 516104 | tf_op jit(solution)/shard_map/ppermute | solution.py:45
  149.1 10.9 %collective-permute-start.35 = (s16[96,896]{1,0:T(8,128)(2,1)S(1)}, s16[96,896]{1,0:T(8,128)(2,1)S(1)}, u32[]{:S(2)}, u32[]{:S(2)}) collective-permute-start(s16[96,896]{1,0:T(8,128)(2,1)S(1)} %get-tuple-element.70), channel_id=1, source_target_pairs={{0,6},{1,7},{2,4},{3,5},{4,2},{5,3},{6,0},{7,1},{8,14},{9,15},{10,... | collective-permute-start | bytes 516104 | tf_op jit(solution)/shard_map/ppermute | solution.py:45
  149.2 11.7 %collective-permute-start.34 = (s16[96,896]{1,0:T(8,128)(2,1)S(1)}, s16[96,896]{1,0:T(8,128)(2,1)S(1)}, u32[]{:S(2)}, u32[]{:S(2)}) collective-permute-start(s16[96,896]{1,0:T(8,128)(2,1)S(1)} %get-tuple-element.70), channel_id=1, source_target_pairs={{0,4},{1,5},{2,6},{3,7},{4,0},{5,1},{6,2},{7,3},{8,12},{9,13},{10,... | collective-permute-start | bytes 516104 | tf_op jit(solution)/shard_map/ppermute | solution.py:45
  150.9 10.0 %collective-permute-start.33 = (s16[96,896]{1,0:T(8,128)(2,1)S(1)}, s16[96,896]{1,0:T(8,128)(2,1)S(1)}, u32[]{:S(2)}, u32[]{:S(2)}) collective-permute-start(s16[96,896]{1,0:T(8,128)(2,1)S(1)} %get-tuple-element.70), channel_id=1, source_target_pairs={{0,2},{1,3},{2,0},{3,1},{4,6},{5,7},{6,4},{7,5},{8,10},{9,11},{10,... | collective-permute-start | bytes 516104 | tf_op jit(solution)/shard_map/ppermute | solution.py:45
  152.5 9.1 %collective-permute-start.36 = (s16[96,896]{1,0:T(8,128)(2,1)S(1)}, s16[96,896]{1,0:T(8,128)(2,1)S(1)}, u32[]{:S(2)}, u32[]{:S(2)}) collective-permute-start(s16[96,896]{1,0:T(8,128)(2,1)S(1)} %get-tuple-element.70), channel_id=1, source_target_pairs={{0,1},{1,0},{2,3},{3,2},{4,5},{5,4},{6,7},{7,6},{8,9},{9,8},{10,11... | collective-permute-start | bytes 516104 | tf_op jit(solution)/shard_map/ppermute | solution.py:45
  160.0 1.9 %collective-permute-start.39 = (s16[96,896]{1,0:T(8,128)(2,1)S(1)}, s16[96,896]{1,0:T(8,128)(2,1)S(1)}, u32[]{:S(2)}, u32[]{:S(2)}) collective-permute-start(s16[96,896]{1,0:T(8,128)(2,1)S(1)} %collective-permute-done.35.refs_7_), channel_id=1, source_target_pairs={{0,1},{1,0},{2,3},{3,2},{4,5},{5,4},{6,7},{7,6},{8,9},{9,8},{10,11... | collective-permute-start | bytes 516104 | tf_op jit(solution)/shard_map/ppermute | solution.py:45
  160.9 1.4 collective-permute-start.38
  160.9 1.7 collective-permute-start.37

commit v2 on v1

--- a/solution.py
+++ b/solution.py
@@ -52,7 +52,8 @@
 def gather(left, upper):
     lefts, uppers = [left], [upper]
     for e in ORDER[1:]:
-        lefts.append(send(left, lambda r, c, p: (r, c ^ e, p)))
+        src, hop = (lefts[1], 1) if e == 3 else (left, e)
+        lefts.append(send(src, lambda r, c, p: (r, c ^ hop, p)))
         uppers.append(send(upper, lambda r, c, p: (r ^ e, c, p)))
     return lefts, uppers
 
@@ -67,7 +68,11 @@
 
 
 def live_block(ids, level, n, slab, i):
-    return ids[level, n, slab * LIVE + i] - slab * SLAB
+    if len(ids.shape) == 1:
+        number = ids[((level - 1) * NODES + n) * SIDE * LIVE + slab * LIVE + i]
+    else:
+        number = ids[level, n, slab * LIVE + i]
+    return number - slab * SLAB
 
 
 def pack0_kernel(ids, role, left, upper, lo, uo, sems):
@@ -431,9 +436,8 @@
         (sds(L2 + L3, 128), sds(2 * U, 128), sds(3 * NUM, 128)), [dma], 4,
         role, own, m1, m2, m3,
     )
-    per = NODES * SIDE * LIVE
-    ids = jnp.stack([nums[j * NUM, j * per : (j + 1) * per] for j in range(3)]).astype(jnp.int32)
-    ids = jnp.concatenate([ids0[:1], ids.reshape(3, NODES, SIDE * LIVE)])
+    lane = jnp.arange(128, dtype=jnp.int32) // (NODES * SIDE * LIVE)
+    ids = sum(jnp.where(lane == j, nums[j * NUM], 0) for j in range(3)).astype(jnp.int32)
     l23, u23 = gather(z23, x23)
 
     half = SLAB * 64

time: 167 us -> 149 us (0.89)
  waiting for transfers between devices: 83.1 us -> 62.1 us
  starting transfers between devices: 50.1 us -> 57.7 us
  local copies, waits for them, and re-layouts: 4.68 us -> 1.29 us
    ppermute x40, waiting for transfers between devices: 83.1 us -> 62.1 us  [send(): return lax.ppermute(x, AXES, pairs)]
    ppermute x40, starting transfers between devices: 50.1 us -> 57.7 us  [send(): return lax.ppermute(x, AXES, pairs)]
    another operation x3 -> x0, local copies, waits for them, and re-layouts: 2.05 us -> none  [on_device(): jnp.stack([nums[j * NUM, j * per:(j + 1) * per] for j in range(3)])]
  transfers between devices with their start and end apart: 40 -> 40, of which waited for: 19 -> 18; matrix products, arithmetic and copies ran while one was open for 2% -> 0% of each run, Pallas kernels for 8% -> 9%
where the time goes in v2:
time: 149 us; the launch traced here: 147 us
  waiting for transfers between devices  62.1 us (42%)
  starting transfers between devices  57.7 us (39%)
  Pallas kernels  25 us (17%)
    ppermute x40, waiting for transfers between devices, send(): return lax.ppermute(x, AXES, pairs)  62.1 us
    ppermute x40, starting transfers between devices, send(): return lax.ppermute(x, AXES, pairs)  57.7 us
    pallas_call x13, Pallas kernels, call(): pl.pallas_call(kernel, out_shape=outs, in_specs=specs, out_specs=jax.tree...  25 us
  transfers between devices with their start and end apart: 40, of which 18 were waited for; matrix products, arithmetic and copies ran while one was open for 0% of the time, Pallas kernels for 9%

profile of v2, /device:TPU:3, one launch (start us, length us, event | category | flops | bytes accessed | tf_op | source)
XLA Modules:
  0.0 147.1 jit_solution(2382492894313362603)
XLA Ops:
  0.6 2.9 %shard_map.46 = (bf16[2,2,384,128]{3,2,1,0:T(8,128)(2,1)}, bf16[2,3,256,128]{3,2,1,0:T(8,128)(2,1)}) custom-call(s32[4,2,12]{2,1,0:T(2,128)} %bitcast.29, s32[4]{0:T(128)} %pad_add_fusion.role, bf16[4,2,1,768,256]{4,3,2,1,0:T(8,128)(2,1)} %left.2, bf16[4,2,1,256,768]{4,3,2,1,0:T(8,128)(2,1)} %upper.2), custom_call_target="tpu_custom_call" | custom-call | flops 1073741824 | bytes 4194304 | tf_op jit(solution)/shard_map/pallas_call | solution.py:371
  3.5 4.5 %shard_map.48 = (bf16[4624,128]{1,0:T(8,128)(2,1)}, bf16[4624,128]{1,0:T(8,128)(2,1)}) custom-call(s32[4,2,12]{2,1,0:T(2,128)} %bitcast.30, s32[4]{0:T(128)} %pad_add_fusion.role, bf16[4,2,1,768,256]{4,3,2,1,0:T(8,128)(2,1)} %left.2, bf16[4,2,1,256,768]{4,3,2,1,0:T(8,128)(2,1)} %upper.2), custom_call_target="tpu_custom_call" | custom-call | flops 1073741824 | bytes 4194304 | tf_op jit(solution)/shard_map/pallas_call | solution.py:371
  8.7 1.6 %collective-permute-start.1 = (bf16[1536,128]{1,0:T(8,128)(2,1)S(1)}, bf16[1536,128]{1,0:T(8,128)(2,1)S(1)}, u32[]{:S(2)}, u32[]{:S(2)}) collective-permute-start(bf16[1536,128]{1,0:T(8,128)(2,1)S(1)} %bitcast.22), channel_id=1, source_target_pairs={{0,16},{1,17},{2,18},{3,19},{4,20},{5,21},{6,22},{7,23},{8,24},{9,... | collective-permute-start | bytes 1179656 | tf_op jit(solution)/shard_map/ppermute | solution.py:45
  10.4 3.0 %collective-permute-start = (bf16[1536,128]{1,0:T(8,128)(2,1)S(1)}, bf16[1536,128]{1,0:T(8,128)(2,1)S(1)}, u32[]{:S(2)}, u32[]{:S(2)}) collective-permute-start(bf16[1536,128]{1,0:T(8,128)(2,1)S(1)} %bitcast.23), channel_id=1, source_target_pairs={{0,32},{1,33},{2,34},{3,35},{4,36},{5,37},{6,38},{7,39},{8,40},{9,... | collective-permute-start | bytes 1179656 | tf_op jit(solution)/shard_map/ppermute | solution.py:45
  13.4 1.2 collective-permute-start.5
  14.6 1.5 %collective-permute-start.4 = (bf16[1536,128]{1,0:T(8,128)(2,1)S(1)}, bf16[1536,128]{1,0:T(8,128)(2,1)S(1)}, u32[]{:S(2)}, u32[]{:S(2)}) collective-permute-start(bf16[1536,128]{1,0:T(8,128)(2,1)S(1)} %bitcast.26), channel_id=1, source_target_pairs={{0,64},{1,65},{2,66},{3,67},{4,68},{5,69},{6,70},{7,71},{8,72},{9,... | collective-permute-start | bytes 1179656 | tf_op jit(solution)/shard_map/ppermute | solution.py:45
  16.1 1.3 copy-done.5
  17.4 3.1 %shard_map.49 = (bf16[2128,128]{1,0:T(8,128)(2,1)S(1)}, bf16[976,128]{1,0:T(8,128)(2,1)S(1)}, bf16[976,128]{1,0:T(8,128)(2,1)S(1)}, bf16[768,128]{1,0:T(8,128)(2...) custom-call(s32[4]{0:T(128)S(1)} %copy-done.4, bf16[4624,128]{1,0:T(8,128)(2,1)S(1)} %copy-done.5, ...), custom_call_target="tpu_custom_call" | custom-call | flops 1073741824 | bytes 4194304 | tf_op jit(solution)/shard_map/pallas_call | solution.py:371
  20.5 7.3 %collective-permute-done.1.refs_2_ = bf16[1536,128]{1,0:T(8,128)(2,1)S(1)} collective-permute-done((bf16[1536,128]{1,0:T(8,128)(2,1)S(1)}, bf16[1536,128]{1,0:T(8,128)(2,1)S(1)}, u32[]{:S(2)}, u32[]{:S(2)}) %collective-permute-start.1) | collective-permute-done | bytes 393248 | tf_op jit(solution)/shard_map/ppermute | solution.py:45
  27.8 1.3 collective-permute-start.8
  29.1 2.0 %collective-permute-start.2 = (bf16[1536,128]{1,0:T(8,128)(2,1)S(1)}, bf16[1536,128]{1,0:T(8,128)(2,1)S(1)}, u32[]{:S(2)}, u32[]{:S(2)}) collective-permute-start(bf16[1536,128]{1,0:T(8,128)(2,1)S(1)} %collective-permute-done.refs_1_), channel_id=1, source_target_pairs={{0,16},{1,17},{2,18},{3,19},{4,20},{5,21},{6,22},{7,23},{8,24},{9,... | collective-permute-start | bytes 1179656 | tf_op jit(solution)/shard_map/ppermute | solution.py:45
  31.1 2.9 %collective-permute-start.9 = (bf16[976,128]{1,0:T(8,128)(2,1)S(1)}, bf16[976,128]{1,0:T(8,128)(2,1)S(1)}, u32[]{:S(2)}, u32[]{:S(2)}) collective-permute-start(bf16[976,128]{1,0:T(8,128)(2,1)S(1)} %get-tuple-element.48), channel_id=1, source_target_pairs={{0,4},{1,5},{2,6},{3,7},{4,0},{5,1},{6,2},{7,3},{8,12},{9,13},{10,... | collective-permute-start | bytes 749576 | tf_op jit(solution)/shard_map/ppermute | solution.py:45
  34.8 2.1 %collective-permute-start.11 = (bf16[768,128]{1,0:T(8,128)(2,1)S(1)}, bf16[768,128]{1,0:T(8,128)(2,1)S(1)}, u32[]{:S(2)}, u32[]{:S(2)}) collective-permute-start(bf16[768,128]{1,0:T(8,128)(2,1)S(1)} %get-tuple-element.51.refs_0_), channel_id=1, source_target_pairs={{0,32},{1,33},{2,34},{3,35},{4,36},{5,37},{6,38},{7,39},{8,40},{9,... | collective-permute-start | bytes 589832 | tf_op jit(solution)/shard_map/ppermute | solution.py:45
  36.9 1.8 %collective-permute-done.2.refs_3_ = bf16[1536,128]{1,0:T(8,128)(2,1)S(1)} collective-permute-done((bf16[1536,128]{1,0:T(8,128)(2,1)S(1)}, bf16[1536,128]{1,0:T(8,128)(2,1)S(1)}, u32[]{:S(2)}, u32[]{:S(2)}) %collective-permute-start.2) | collective-permute-done | bytes 393248 | tf_op jit(solution)/shard_map/ppermute | solution.py:45
  38.8 2.5 %shard_map.47.t0 = f32[768,768]{1,0:T(8,128)S(1)} custom-call(s32[4,2,12]{2,1,0:T(2,128)S(1)} %bitcast.31, s32[4]{0:T(128)S(1)} %copy-done.4, f32[768,768]{1,0:T(8,128)S(1)} %bitcast.21, bf16[1536,128]{1,0:T(8,128)(2,1)S(1)} %bitcast.24, bf16[1536,128]{1,0:T(8,128)(2,1)S(1)} %collective-permute-done.refs_1_, ...), custom_call_target="tpu_custom_call" | custom-call | flops 1073741824 | bytes 4194304 | tf_op jit(solution)/shard_map/pallas_call | solution.py:371
  41.3 2.3 %collective-permute-start.12 = (bf16[768,128]{1,0:T(8,128)(2,1)S(1)}, bf16[768,128]{1,0:T(8,128)(2,1)S(1)}, u32[]{:S(2)}, u32[]{:S(2)}) collective-permute-start(bf16[768,128]{1,0:T(8,128)(2,1)S(1)} %get-tuple-element.51.refs_0_), channel_id=1, source_target_pairs={{0,16},{1,17},{2,18},{3,19},{4,20},{5,21},{6,22},{7,23},{8,24},{9,... | collective-permute-start | bytes 589832 | tf_op jit(solution)/shard_map/ppermute | solution.py:45
  43.6 1.2 collective-permute-start.16
  44.8 4.0 %collective-permute-done.9.m2 = bf16[976,128]{1,0:T(8,128)(2,1)S(1)} collective-permute-done((bf16[976,128]{1,0:T(8,128)(2,1)S(1)}, bf16[976,128]{1,0:T(8,128)(2,1)S(1)}, u32[]{:S(2)}, u32[]{:S(2)}) %collective-permute-start.9) | collective-permute-done | bytes 249888 | tf_op jit(solution)/shard_map/ppermute | solution.py:45
  49.0 2.1 %collective-permute-start.14 = (bf16[768,128]{1,0:T(8,128)(2,1)S(1)}, bf16[768,128]{1,0:T(8,128)(2,1)S(1)}, u32[]{:S(2)}, u32[]{:S(2)}) collective-permute-start(bf16[768,128]{1,0:T(8,128)(2,1)S(1)} %get-tuple-element.52.refs_4_), channel_id=1, source_target_pairs={{0,128},{1,129},{2,130},{3,131},{4,132},{5,133},{6,134},{7,135},{8... | collective-permute-start | bytes 589832 | tf_op jit(solution)/shard_map/ppermute | solution.py:45
  51.2 1.5 %shard_map.50 = (bf16[576,128]{1,0:T(8,128)(2,1)S(1)}, bf16[1536,128]{1,0:T(8,128)(2,1)S(1)}, bf16[48,128]{1,0:T(8,128)(2,1)S(1)}) custom-call(s32[4]{0:T(128)S(1)} %copy-done.4, bf16[2128,128]{1,0:T(8,128)(2,1)S(1)} %get-tuple-element.46.own, bf16[2128,128]{1,0:T(8,128)(2,1)S(1)} %collective-permute-done.8.m1, ...), custom_call_target="tpu_custom_call" | custom-call | flops 1073741824 | bytes 4194304 | tf_op jit(solution)/shard_map/pallas_call | solution.py:371
  53.6 4.9 %collective-permute-done.14.refs_5_ = bf16[768,128]{1,0:T(8,128)(2,1)S(1)} collective-permute-done((bf16[768,128]{1,0:T(8,128)(2,1)S(1)}, bf16[768,128]{1,0:T(8,128)(2,1)S(1)}, u32[]{:S(2)}, u32[]{:S(2)}) %collective-permute-start.14) | collective-permute-done | bytes 196640 | tf_op jit(solution)/shard_map/ppermute | solution.py:45
  58.5 1.8 %shard_map.51 = (f32[384,768]{1,0:T(8,128)S(1)}, f32[384,768]{1,0:T(8,128)S(1)}) custom-call(s32[128]{0:T(128)S(1)} %fusion.2.ids, s32[4]{0:T(128)S(1)} %copy-done.4, f32[768,768]{1,0:T(8,128)S(1)} %shard_map.47.t0, bf16[768,128]{1,0:T(8,128)(2,1)S(1)} %get-tuple-element.51.refs_0_, bf16[768,128]{1,0:T(8,128)(2,1)S(1)} %collective-permute-done.11.refs_1_, ...), custom_call_target="tpu_custom_call" | custom-call | flops 1073741824 | bytes 4194304 | tf_op jit(solution)/shard_map/pallas_call | solution.py:371
  60.3 2.9 %collective-permute-start.17 = (f32[384,768]{1,0:T(8,128)S(1)}, f32[384,768]{1,0:T(8,128)S(1)}, u32[]{:S(2)}, u32[]{:S(2)}) collective-permute-start(f32[384,768]{1,0:T(8,128)S(1)} %get-tuple-element.54), channel_id=1, source_target_pairs={{0,1},{1,0},{2,3},{3,2},{4,5},{5,4},{6,7},{7,6},{8,9},{9,8},{10,11... | collective-permute-start | bytes 3538952 | tf_op jit(solution)/shard_map/ppermute | solution.py:45
  63.3 2.6 %collective-permute-start.19 = (bf16[576,128]{1,0:T(8,128)(2,1)S(1)}, bf16[576,128]{1,0:T(8,128)(2,1)S(1)}, u32[]{:S(2)}, u32[]{:S(2)}) collective-permute-start(bf16[576,128]{1,0:T(8,128)(2,1)S(1)} %get-tuple-element.57.refs_0_), channel_id=1, source_target_pairs={{0,32},{1,33},{2,34},{3,35},{4,36},{5,37},{6,38},{7,39},{8,40},{9,... | collective-permute-start | bytes 442376 | tf_op jit(solution)/shard_map/ppermute | solution.py:45
  66.3 5.1 %collective-permute-done.20.refs_2_ = bf16[576,128]{1,0:T(8,128)(2,1)S(1)} collective-permute-done((bf16[576,128]{1,0:T(8,128)(2,1)S(1)}, bf16[576,128]{1,0:T(8,128)(2,1)S(1)}, u32[]{:S(2)}, u32[]{:S(2)}) %collective-permute-start.20) | collective-permute-done | bytes 147488 | tf_op jit(solution)/shard_map/ppermute | solution.py:45
  71.4 1.3 collective-permute-start.23
  72.9 2.4 %collective-permute-start.21 = (bf16[576,128]{1,0:T(8,128)(2,1)S(1)}, bf16[576,128]{1,0:T(8,128)(2,1)S(1)}, u32[]{:S(2)}, u32[]{:S(2)}) collective-permute-start(bf16[576,128]{1,0:T(8,128)(2,1)S(1)} %collective-permute-done.19.refs_1_), channel_id=1, source_target_pairs={{0,16},{1,17},{2,18},{3,19},{4,20},{5,21},{6,22},{7,23},{8,24},{9,... | collective-permute-start | bytes 442376 | tf_op jit(solution)/shard_map/ppermute | solution.py:45
  76.3 1.8 %collective-permute-done.21.refs_3_ = bf16[576,128]{1,0:T(8,128)(2,1)S(1)} collective-permute-done((bf16[576,128]{1,0:T(8,128)(2,1)S(1)}, bf16[576,128]{1,0:T(8,128)(2,1)S(1)}, u32[]{:S(2)}, u32[]{:S(2)}) %collective-permute-start.21) | collective-permute-done | bytes 147488 | tf_op jit(solution)/shard_map/ppermute | solution.py:45
  78.1 1.6 %collective-permute-start.18 = (s16[192,896]{1,0:T(8,128)(2,1)S(1)}, s16[192,896]{1,0:T(8,128)(2,1)S(1)}, u32[]{:S(2)}, u32[]{:S(2)}) collective-permute-start(s16[192,896]{1,0:T(8,128)(2,1)S(1)} %get-tuple-element.56), channel_id=1, source_target_pairs={{0,2},{1,3},{2,0},{3,1},{4,6},{5,7},{6,4},{7,5},{8,10},{9,11},{10,... | collective-permute-start | bytes 1032200 | tf_op jit(solution)/shard_map/ppermute | solution.py:45
  80.8 8.4 %collective-permute-done.22.refs_5_ = bf16[1536,128]{1,0:T(8,128)(2,1)S(1)} collective-permute-done((bf16[1536,128]{1,0:T(8,128)(2,1)S(1)}, bf16[1536,128]{1,0:T(8,128)(2,1)S(1)}, u32[]{:S(2)}, u32[]{:S(2)}) %collective-permute-start.22) | collective-permute-done | bytes 393248 | tf_op jit(solution)/shard_map/ppermute | solution.py:45
  89.2 1.7 %shard_map.53 = (f32[144,384]{1,0:T(8,128)S(1)}, f32[144,384]{1,0:T(8,128)S(1)}) custom-call(s32[4]{0:T(128)S(1)} %copy-done.4, bf16[576,128]{1,0:T(8,128)(2,1)S(1)} %get-tuple-element.57.refs_0_, bf16[576,128]{1,0:T(8,128)(2,1)S(1)} %collective-permute-done.19.refs_1_, bf16[576,128]{1,0:T(8,128)(2,1)S(1)} %collective-permute-done.20.refs_2_, ...), custom_call_target="tpu_custom_call" | custom-call | flops 1073741824 | bytes 4194304 | tf_op jit(solution)/shard_map/pallas_call | solution.py:371
  90.9 2.2 %collective-permute-start.25 = (f32[144,384]{1,0:T(8,128)S(1)}, f32[144,384]{1,0:T(8,128)S(1)}, u32[]{:S(2)}, u32[]{:S(2)}) collective-permute-start(f32[144,384]{1,0:T(8,128)S(1)} %get-tuple-element.60), channel_id=1, source_target_pairs={{0,1},{1,0},{2,3},{3,2},{4,5},{5,4},{6,7},{7,6},{8,9},{9,8},{10,11... | collective-permute-start | bytes 663560 | tf_op jit(solution)/shard_map/ppermute | solution.py:45
  93.1 1.1 collective-permute-done.25.theirs
  95.7 6.8 %collective-permute-done.27.b = s16[96,896]{1,0:T(8,128)(2,1)S(1)} collective-permute-done((s16[96,896]{1,0:T(8,128)(2,1)S(1)}, s16[96,896]{1,0:T(8,128)(2,1)S(1)}, u32[]{:S(2)}, u32[]{:S(2)}) %collective-permute-start.27) | collective-permute-done | bytes 172064 | tf_op jit(solution)/shard_map/ppermute | solution.py:45
  103.4 2.0 %collective-permute-start.29 = (s16[96,896]{1,0:T(8,128)(2,1)S(1)}, s16[96,896]{1,0:T(8,128)(2,1)S(1)}, u32[]{:S(2)}, u32[]{:S(2)}) collective-permute-start(s16[96,896]{1,0:T(8,128)(2,1)S(1)} %get-tuple-element.66.s2), channel_id=1, source_target_pairs={{0,4},{1,5},{2,6},{3,7},{4,0},{5,1},{6,2},{7,3},{8,12},{9,13},{10,... | collective-permute-start | bytes 516104 | tf_op jit(solution)/shard_map/ppermute | solution.py:45
  105.4 1.3 collective-permute-start.28
  106.6 2.2 %collective-permute-done.30.refs_2_ = s16[96,896]{1,0:T(8,128)(2,1)S(1)} collective-permute-done((s16[96,896]{1,0:T(8,128)(2,1)S(1)}, s16[96,896]{1,0:T(8,128)(2,1)S(1)}, u32[]{:S(2)}, u32[]{:S(2)}) %collective-permute-start.30) | collective-permute-done | bytes 172064 | tf_op jit(solution)/shard_map/ppermute | solution.py:45
  108.8 4.7 %collective-permute-done.29.refs_1_ = s16[96,896]{1,0:T(8,128)(2,1)S(1)} collective-permute-done((s16[96,896]{1,0:T(8,128)(2,1)S(1)}, s16[96,896]{1,0:T(8,128)(2,1)S(1)}, u32[]{:S(2)}, u32[]{:S(2)}) %collective-permute-start.29) | collective-permute-done | bytes 172064 | tf_op jit(solution)/shard_map/ppermute | solution.py:45
  113.5 1.5 shard_map.56
  115.0 2.3 %collective-permute-start.31 = (s16[384,896]{1,0:T(8,128)(2,1)S(1)}, s16[384,896]{1,0:T(8,128)(2,1)S(1)}, u32[]{:S(2)}, u32[]{:S(2)}) collective-permute-start(s16[384,896]{1,0:T(8,128)(2,1)S(1)} %shard_map.56), channel_id=1, source_target_pairs={{0,1},{1,0},{2,3},{3,2},{4,5},{5,4},{6,7},{7,6},{8,9},{9,8},{10,11... | collective-permute-start | bytes 2064392 | tf_op jit(solution)/shard_map/ppermute | solution.py:45
  117.3 5.9 %collective-permute-start.32 = (s16[96,896]{1,0:T(8,128)(2,1)S(1)}, s16[96,896]{1,0:T(8,128)(2,1)S(1)}, u32[]{:S(2)}, u32[]{:S(2)}) collective-permute-start(s16[96,896]{1,0:T(8,128)(2,1)S(1)} %get-tuple-element.68), channel_id=1, source_target_pairs={{0,8},{1,9},{2,10},{3,11},{4,12},{5,13},{6,14},{7,15},{8,0},{9,1},... | collective-permute-start | bytes 516104 | tf_op jit(solution)/shard_map/ppermute | solution.py:45
  123.2 7.5 %collective-permute-done.32.r = s16[96,896]{1,0:T(8,128)(2,1)S(1)} collective-permute-done((s16[96,896]{1,0:T(8,128)(2,1)S(1)}, s16[96,896]{1,0:T(8,128)(2,1)S(1)}, u32[]{:S(2)}, u32[]{:S(2)}) %collective-permute-start.32) | collective-permute-done | bytes 172064 | tf_op jit(solution)/shard_map/ppermute | solution.py:45
  130.9 1.2 collective-permute-start.35
  132.2 1.1 collective-permute-start.34
  134.3 1.9 %collective-permute-start.36 = (s16[96,896]{1,0:T(8,128)(2,1)S(1)}, s16[96,896]{1,0:T(8,128)(2,1)S(1)}, u32[]{:S(2)}, u32[]{:S(2)}) collective-permute-start(s16[96,896]{1,0:T(8,128)(2,1)S(1)} %get-tuple-element.70), channel_id=1, source_target_pairs={{0,1},{1,0},{2,3},{3,2},{4,5},{5,4},{6,7},{7,6},{8,9},{9,8},{10,11... | collective-permute-start | bytes 516104 | tf_op jit(solution)/shard_map/ppermute | solution.py:45
  136.2 3.4 %collective-permute-done.35.refs_7_ = s16[96,896]{1,0:T(8,128)(2,1)S(1)} collective-permute-done((s16[96,896]{1,0:T(8,128)(2,1)S(1)}, s16[96,896]{1,0:T(8,128)(2,1)S(1)}, u32[]{:S(2)}, u32[]{:S(2)}) %collective-permute-start.35) | collective-permute-done | bytes 172064 | tf_op jit(solution)/shard_map/ppermute | solution.py:45
  139.6 3.1 %collective-permute-start.39 = (s16[96,896]{1,0:T(8,128)(2,1)S(1)}, s16[96,896]{1,0:T(8,128)(2,1)S(1)}, u32[]{:S(2)}, u32[]{:S(2)}) collective-permute-start(s16[96,896]{1,0:T(8,128)(2,1)S(1)} %collective-permute-done.35.refs_7_), channel_id=1, source_target_pairs={{0,1},{1,0},{2,3},{3,2},{4,5},{5,4},{6,7},{7,6},{8,9},{9,8},{10,11... | collective-permute-start | bytes 516104 | tf_op jit(solution)/shard_map/ppermute | solution.py:45
  144.4 2.5 %shard_map.58 = f32[768,768]{1,0:T(8,128)} custom-call(s32[4]{0:T(128)S(1)} %copy-done.4, f32[768,768]{1,0:T(8,128)S(1)} %shard_map.47.t0, f32[768,768]{1,0:T(8,128)S(1)} %collective-permute-done.6.r0, f32[192,768]{1,0:T(8,128)S(1)} %get-tuple-element.61.s1, s16[192,896]{1,0:T(8,128)(2,1)S(1)} %collective-permute-done.26.r1, ...), custom_call_target="tpu_custom_call" | custom-call | flops 1073741824 | bytes 4194304 | tf_op jit(solution)/shard_map/pallas_call | solution.py:371
  (59 shorter events, 11.3 us)
Async XLA Ops:
  3.4 5.3 %copy-start.1 = (bf16[2,2,384,128]{3,2,1,0:T(8,128)(2,1)S(1)}, bf16[2,2,384,128]{3,2,1,0:T(8,128)(2,1)}, u32[]{:S(2)}) copy-start(bf16[2,2,384,128]{3,2,1,0:T(8,128)(2,1)} %get-tuple-element.38) | copy-start | bytes 1179652
  3.5 9.9 %copy-start.2 = (bf16[2,3,256,128]{3,2,1,0:T(8,128)(2,1)S(1)}, bf16[2,3,256,128]{3,2,1,0:T(8,128)(2,1)}, u32[]{:S(2)}) copy-start(bf16[2,3,256,128]{3,2,1,0:T(8,128)(2,1)} %get-tuple-element.39) | copy-start | bytes 1179652
  3.5 12.6 %copy-start.4 = (s32[4]{0:T(128)S(1)}, s32[4]{0:T(128)}, u32[]{:S(2)}) copy-start(s32[4]{0:T(128)} %pad_add_fusion.role) | copy-start | bytes 52
  7.9 30.8 %copy-start = (f32[1,768,768]{2,1,0:T(8,128)S(1)}, f32[1,768,768]{2,1,0:T(8,128)}, u32[]{:S(2)}) copy-start(f32[1,768,768]{2,1,0:T(8,128)} %param.4) | copy-start | bytes 7077892
  8.0 30.8 %copy-start.3 = (s32[4,2,1,12]{3,2,1,0:T(1,128)S(1)}, s32[4,2,1,12]{3,2,1,0:T(1,128)}, u32[]{:S(2)}) copy-start(s32[4,2,1,12]{3,2,1,0:T(1,128)} %param.7) | copy-start | bytes 1156
  8.0 8.1 %collective-permute-start.7 = (bf16[4624,128]{1,0:T(8,128)(2,1)}, bf16[4624,128]{1,0:T(8,128)(2,1)S(1)}, u32[]{:S(2)}, u32[]{:S(2)}) collective-permute-start(bf16[4624,128]{1,0:T(8,128)(2,1)} %get-tuple-element.45), channel_id=1, source_target_pairs={{0,1},{1,0},{2,3},{3,2},{4,5},{5,4},{6,7},{7,6},{8,9},{9,8},{10,11... | collective-permute-start | bytes 3551240 | tf_op jit(solution)/shard_map/ppermute | solution.py:45
  8.7 19.1 %collective-permute-start.1 = (bf16[1536,128]{1,0:T(8,128)(2,1)S(1)}, bf16[1536,128]{1,0:T(8,128)(2,1)S(1)}, u32[]{:S(2)}, u32[]{:S(2)}) collective-permute-start(bf16[1536,128]{1,0:T(8,128)(2,1)S(1)} %bitcast.22), channel_id=1, source_target_pairs={{0,16},{1,17},{2,18},{3,19},{4,20},{5,21},{6,22},{7,23},{8,24},{9,... | collective-permute-start | bytes 1179656 | tf_op jit(solution)/shard_map/ppermute | solution.py:45
  10.4 18.8 %collective-permute-start = (bf16[1536,128]{1,0:T(8,128)(2,1)S(1)}, bf16[1536,128]{1,0:T(8,128)(2,1)S(1)}, u32[]{:S(2)}, u32[]{:S(2)}) collective-permute-start(bf16[1536,128]{1,0:T(8,128)(2,1)S(1)} %bitcast.23), channel_id=1, source_target_pairs={{0,32},{1,33},{2,34},{3,35},{4,36},{5,37},{6,38},{7,39},{8,40},{9,... | collective-permute-start | bytes 1179656 | tf_op jit(solution)/shard_map/ppermute | solution.py:45
  13.4 17.8 %collective-permute-start.5 = (bf16[1536,128]{1,0:T(8,128)(2,1)S(1)}, bf16[1536,128]{1,0:T(8,128)(2,1)S(1)}, u32[]{:S(2)}, u32[]{:S(2)}) collective-permute-start(bf16[1536,128]{1,0:T(8,128)(2,1)S(1)} %bitcast.25), channel_id=1, source_target_pairs={{0,192},{1,193},{2,194},{3,195},{4,196},{5,197},{6,198},{7,199},{8... | collective-permute-start | bytes 1179656 | tf_op jit(solution)/shard_map/ppermute | solution.py:45
  14.6 19.5 %collective-permute-start.4 = (bf16[1536,128]{1,0:T(8,128)(2,1)S(1)}, bf16[1536,128]{1,0:T(8,128)(2,1)S(1)}, u32[]{:S(2)}, u32[]{:S(2)}) collective-permute-start(bf16[1536,128]{1,0:T(8,128)(2,1)S(1)} %bitcast.26), channel_id=1, source_target_pairs={{0,64},{1,65},{2,66},{3,67},{4,68},{5,69},{6,70},{7,71},{8,72},{9,... | collective-permute-start | bytes 1179656 | tf_op jit(solution)/shard_map/ppermute | solution.py:45
  16.1 18.7 %collective-permute-start.3 = (bf16[1536,128]{1,0:T(8,128)(2,1)S(1)}, bf16[1536,128]{1,0:T(8,128)(2,1)S(1)}, u32[]{:S(2)}, u32[]{:S(2)}) collective-permute-start(bf16[1536,128]{1,0:T(8,128)(2,1)S(1)} %bitcast.27), channel_id=1, source_target_pairs={{0,128},{1,129},{2,130},{3,131},{4,132},{5,133},{6,134},{7,135},{8... | collective-permute-start | bytes 1179656 | tf_op jit(solution)/shard_map/ppermute | solution.py:45
  16.1 1.3 copy-start.5
  27.8 23.3 %collective-permute-start.8 = (bf16[2128,128]{1,0:T(8,128)(2,1)S(1)}, bf16[2128,128]{1,0:T(8,128)(2,1)S(1)}, u32[]{:S(2)}, u32[]{:S(2)}) collective-permute-start(bf16[2128,128]{1,0:T(8,128)(2,1)S(1)} %get-tuple-element.47), channel_id=1, source_target_pairs={{0,2},{1,3},{2,0},{3,1},{4,6},{5,7},{6,4},{7,5},{8,10},{9,11},{10,... | collective-permute-start | bytes 1634312 | tf_op jit(solution)/shard_map/ppermute | solution.py:45
  29.1 9.6 %collective-permute-start.2 = (bf16[1536,128]{1,0:T(8,128)(2,1)S(1)}, bf16[1536,128]{1,0:T(8,128)(2,1)S(1)}, u32[]{:S(2)}, u32[]{:S(2)}) collective-permute-start(bf16[1536,128]{1,0:T(8,128)(2,1)S(1)} %collective-permute-done.refs_1_), channel_id=1, source_target_pairs={{0,16},{1,17},{2,18},{3,19},{4,20},{5,21},{6,22},{7,23},{8,24},{9,... | collective-permute-start | bytes 1179656 | tf_op jit(solution)/shard_map/ppermute | solution.py:45
  31.1 17.7 %collective-permute-start.9 = (bf16[976,128]{1,0:T(8,128)(2,1)S(1)}, bf16[976,128]{1,0:T(8,128)(2,1)S(1)}, u32[]{:S(2)}, u32[]{:S(2)}) collective-permute-start(bf16[976,128]{1,0:T(8,128)(2,1)S(1)} %get-tuple-element.48), channel_id=1, source_target_pairs={{0,4},{1,5},{2,6},{3,7},{4,0},{5,1},{6,2},{7,3},{8,12},{9,13},{10,... | collective-permute-start | bytes 749576 | tf_op jit(solution)/shard_map/ppermute | solution.py:45
  34.0 15.0 %collective-permute-start.10 = (bf16[976,128]{1,0:T(8,128)(2,1)S(1)}, bf16[976,128]{1,0:T(8,128)(2,1)S(1)}, u32[]{:S(2)}, u32[]{:S(2)}) collective-permute-start(bf16[976,128]{1,0:T(8,128)(2,1)S(1)} %get-tuple-element.49), channel_id=1, source_target_pairs={{0,6},{1,7},{2,4},{3,5},{4,2},{5,3},{6,0},{7,1},{8,14},{9,15},{10,... | collective-permute-start | bytes 749576 | tf_op jit(solution)/shard_map/ppermute | solution.py:45
  34.8 8.8 %collective-permute-start.11 = (bf16[768,128]{1,0:T(8,128)(2,1)S(1)}, bf16[768,128]{1,0:T(8,128)(2,1)S(1)}, u32[]{:S(2)}, u32[]{:S(2)}) collective-permute-start(bf16[768,128]{1,0:T(8,128)(2,1)S(1)} %get-tuple-element.51.refs_0_), channel_id=1, source_target_pairs={{0,32},{1,33},{2,34},{3,35},{4,36},{5,37},{6,38},{7,39},{8,40},{9,... | collective-permute-start | bytes 589832 | tf_op jit(solution)/shard_map/ppermute | solution.py:45
  41.3 11.4 %collective-permute-start.12 = (bf16[768,128]{1,0:T(8,128)(2,1)S(1)}, bf16[768,128]{1,0:T(8,128)(2,1)S(1)}, u32[]{:S(2)}, u32[]{:S(2)}) collective-permute-start(bf16[768,128]{1,0:T(8,128)(2,1)S(1)} %get-tuple-element.51.refs_0_), channel_id=1, source_target_pairs={{0,16},{1,17},{2,18},{3,19},{4,20},{5,21},{6,22},{7,23},{8,24},{9,... | collective-permute-start | bytes 589832 | tf_op jit(solution)/shard_map/ppermute | solution.py:45
  43.6 9.1 %collective-permute-start.16 = (bf16[768,128]{1,0:T(8,128)(2,1)S(1)}, bf16[768,128]{1,0:T(8,128)(2,1)S(1)}, u32[]{:S(2)}, u32[]{:S(2)}) collective-permute-start(bf16[768,128]{1,0:T(8,128)(2,1)S(1)} %get-tuple-element.52.refs_4_), channel_id=1, source_target_pairs={{0,192},{1,193},{2,194},{3,195},{4,196},{5,197},{6,198},{7,199},{8... | collective-permute-start | bytes 589832 | tf_op jit(solution)/shard_map/ppermute | solution.py:45
  48.8 4.8 %collective-permute-start.15 = (bf16[768,128]{1,0:T(8,128)(2,1)S(1)}, bf16[768,128]{1,0:T(8,128)(2,1)S(1)}, u32[]{:S(2)}, u32[]{:S(2)}) collective-permute-start(bf16[768,128]{1,0:T(8,128)(2,1)S(1)} %get-tuple-element.52.refs_4_), channel_id=1, source_target_pairs={{0,64},{1,65},{2,66},{3,67},{4,68},{5,69},{6,70},{7,71},{8,72},{9,... | collective-permute-start | bytes 589832 | tf_op jit(solution)/shard_map/ppermute | solution.py:45
  49.0 9.4 %collective-permute-start.14 = (bf16[768,128]{1,0:T(8,128)(2,1)S(1)}, bf16[768,128]{1,0:T(8,128)(2,1)S(1)}, u32[]{:S(2)}, u32[]{:S(2)}) collective-permute-start(bf16[768,128]{1,0:T(8,128)(2,1)S(1)} %get-tuple-element.52.refs_4_), channel_id=1, source_target_pairs={{0,128},{1,129},{2,130},{3,131},{4,132},{5,133},{6,134},{7,135},{8... | collective-permute-start | bytes 589832 | tf_op jit(solution)/shard_map/ppermute | solution.py:45
  51.2 7.3 %collective-permute-start.13 = (bf16[768,128]{1,0:T(8,128)(2,1)S(1)}, bf16[768,128]{1,0:T(8,128)(2,1)S(1)}, u32[]{:S(2)}, u32[]{:S(2)}) collective-permute-start(bf16[768,128]{1,0:T(8,128)(2,1)S(1)} %collective-permute-done.11.refs_1_), channel_id=1, source_target_pairs={{0,16},{1,17},{2,18},{3,19},{4,20},{5,21},{6,22},{7,23},{8,24},{9,... | collective-permute-start | bytes 589832 | tf_op jit(solution)/shard_map/ppermute | solution.py:45
  60.3 12.6 %collective-permute-start.17 = (f32[384,768]{1,0:T(8,128)S(1)}, f32[384,768]{1,0:T(8,128)S(1)}, u32[]{:S(2)}, u32[]{:S(2)}) collective-permute-start(f32[384,768]{1,0:T(8,128)S(1)} %get-tuple-element.54), channel_id=1, source_target_pairs={{0,1},{1,0},{2,3},{3,2},{4,5},{5,4},{6,7},{7,6},{8,9},{9,8},{10,11... | collective-permute-start | bytes 3538952 | tf_op jit(solution)/shard_map/ppermute | solution.py:45
  63.2 71.1 %collective-permute-start.6 = (f32[768,768]{1,0:T(8,128)S(1)}, f32[768,768]{1,0:T(8,128)S(1)}, u32[]{:S(2)}, u32[]{:S(2)}) collective-permute-start(f32[768,768]{1,0:T(8,128)S(1)} %shard_map.47.t0), channel_id=1, source_target_pairs={{0,1},{1,0},{2,3},{3,2},{4,5},{5,4},{6,7},{7,6},{8,9},{9,8},{10,11... | collective-permute-start | bytes 7077896 | tf_op jit(solution)/shard_map/ppermute | solution.py:45
  63.3 8.2 %collective-permute-start.20 = (bf16[576,128]{1,0:T(8,128)(2,1)S(1)}, bf16[576,128]{1,0:T(8,128)(2,1)S(1)}, u32[]{:S(2)}, u32[]{:S(2)}) collective-permute-start(bf16[576,128]{1,0:T(8,128)(2,1)S(1)} %get-tuple-element.57.refs_0_), channel_id=1, source_target_pairs={{0,16},{1,17},{2,18},{3,19},{4,20},{5,21},{6,22},{7,23},{8,24},{9,... | collective-permute-start | bytes 442376 | tf_op jit(solution)/shard_map/ppermute | solution.py:45
  63.3 9.5 %collective-permute-start.19 = (bf16[576,128]{1,0:T(8,128)(2,1)S(1)}, bf16[576,128]{1,0:T(8,128)(2,1)S(1)}, u32[]{:S(2)}, u32[]{:S(2)}) collective-permute-start(bf16[576,128]{1,0:T(8,128)(2,1)S(1)} %get-tuple-element.57.refs_0_), channel_id=1, source_target_pairs={{0,32},{1,33},{2,34},{3,35},{4,36},{5,37},{6,38},{7,39},{8,40},{9,... | collective-permute-start | bytes 442376 | tf_op jit(solution)/shard_map/ppermute | solution.py:45
  65.8 13.9 %collective-permute-start.24 = (bf16[1536,128]{1,0:T(8,128)(2,1)S(1)}, bf16[1536,128]{1,0:T(8,128)(2,1)S(1)}, u32[]{:S(2)}, u32[]{:S(2)}) collective-permute-start(bf16[1536,128]{1,0:T(8,128)(2,1)S(1)} %get-tuple-element.58.refs_4_), channel_id=1, source_target_pairs={{0,192},{1,193},{2,194},{3,195},{4,196},{5,197},{6,198},{7,199},{8... | collective-permute-start | bytes 1179656 | tf_op jit(solution)/shard_map/ppermute | solution.py:45
  71.4 9.4 %collective-permute-start.23 = (bf16[1536,128]{1,0:T(8,128)(2,1)S(1)}, bf16[1536,128]{1,0:T(8,128)(2,1)S(1)}, u32[]{:S(2)}, u32[]{:S(2)}) collective-permute-start(bf16[1536,128]{1,0:T(8,128)(2,1)S(1)} %get-tuple-element.58.refs_4_), channel_id=1, source_target_pairs={{0,64},{1,65},{2,66},{3,67},{4,68},{5,69},{6,70},{7,71},{8,72},{9,... | collective-permute-start | bytes 1179656 | tf_op jit(solution)/shard_map/ppermute | solution.py:45
  72.7 16.5 %collective-permute-start.22 = (bf16[1536,128]{1,0:T(8,128)(2,1)S(1)}, bf16[1536,128]{1,0:T(8,128)(2,1)S(1)}, u32[]{:S(2)}, u32[]{:S(2)}) collective-permute-start(bf16[1536,128]{1,0:T(8,128)(2,1)S(1)} %get-tuple-element.58.refs_4_), channel_id=1, source_target_pairs={{0,128},{1,129},{2,130},{3,131},{4,132},{5,133},{6,134},{7,135},{8... | collective-permute-start | bytes 1179656 | tf_op jit(solution)/shard_map/ppermute | solution.py:45
  72.9 5.2 %collective-permute-start.21 = (bf16[576,128]{1,0:T(8,128)(2,1)S(1)}, bf16[576,128]{1,0:T(8,128)(2,1)S(1)}, u32[]{:S(2)}, u32[]{:S(2)}) collective-permute-start(bf16[576,128]{1,0:T(8,128)(2,1)S(1)} %collective-permute-done.19.refs_1_), channel_id=1, source_target_pairs={{0,16},{1,17},{2,18},{3,19},{4,20},{5,21},{6,22},{7,23},{8,24},{9,... | collective-permute-start | bytes 442376 | tf_op jit(solution)/shard_map/ppermute | solution.py:45
  78.1 16.2 %collective-permute-start.18 = (s16[192,896]{1,0:T(8,128)(2,1)S(1)}, s16[192,896]{1,0:T(8,128)(2,1)S(1)}, u32[]{:S(2)}, u32[]{:S(2)}) collective-permute-start(s16[192,896]{1,0:T(8,128)(2,1)S(1)} %get-tuple-element.56), channel_id=1, source_target_pairs={{0,2},{1,3},{2,0},{3,1},{4,6},{5,7},{6,4},{7,5},{8,10},{9,11},{10,... | collective-permute-start | bytes 1032200 | tf_op jit(solution)/shard_map/ppermute | solution.py:45
  90.9 3.3 %collective-permute-start.25 = (f32[144,384]{1,0:T(8,128)S(1)}, f32[144,384]{1,0:T(8,128)S(1)}, u32[]{:S(2)}, u32[]{:S(2)}) collective-permute-start(f32[144,384]{1,0:T(8,128)S(1)} %get-tuple-element.60), channel_id=1, source_target_pairs={{0,1},{1,0},{2,3},{3,2},{4,5},{5,4},{6,7},{7,6},{8,9},{9,8},{10,11... | collective-permute-start | bytes 663560 | tf_op jit(solution)/shard_map/ppermute | solution.py:45
  95.3 7.1 %collective-permute-start.27 = (s16[96,896]{1,0:T(8,128)(2,1)S(1)}, s16[96,896]{1,0:T(8,128)(2,1)S(1)}, u32[]{:S(2)}, u32[]{:S(2)}) collective-permute-start(s16[96,896]{1,0:T(8,128)(2,1)S(1)} %get-tuple-element.64), channel_id=1, source_target_pairs={{0,4},{1,5},{2,6},{3,7},{4,0},{5,1},{6,2},{7,3},{8,12},{9,13},{10,... | collective-permute-start | bytes 516104 | tf_op jit(solution)/shard_map/ppermute | solution.py:45
  95.4 18.2 %collective-permute-start.26 = (s16[192,896]{1,0:T(8,128)(2,1)S(1)}, s16[192,896]{1,0:T(8,128)(2,1)S(1)}, u32[]{:S(2)}, u32[]{:S(2)}) collective-permute-start(s16[192,896]{1,0:T(8,128)(2,1)S(1)} %get-tuple-element.62.s1), channel_id=1, source_target_pairs={{0,2},{1,3},{2,0},{3,1},{4,6},{5,7},{6,4},{7,5},{8,10},{9,11},{10,... | collective-permute-start | bytes 1032200 | tf_op jit(solution)/shard_map/ppermute | solution.py:45
  103.3 5.6 %collective-permute-start.30 = (s16[96,896]{1,0:T(8,128)(2,1)S(1)}, s16[96,896]{1,0:T(8,128)(2,1)S(1)}, u32[]{:S(2)}, u32[]{:S(2)}) collective-permute-start(s16[96,896]{1,0:T(8,128)(2,1)S(1)} %get-tuple-element.66.s2), channel_id=1, source_target_pairs={{0,6},{1,7},{2,4},{3,5},{4,2},{5,3},{6,0},{7,1},{8,14},{9,15},{10,... | collective-permute-start | bytes 516104 | tf_op jit(solution)/shard_map/ppermute | solution.py:45
  103.4 10.1 %collective-permute-start.29 = (s16[96,896]{1,0:T(8,128)(2,1)S(1)}, s16[96,896]{1,0:T(8,128)(2,1)S(1)}, u32[]{:S(2)}, u32[]{:S(2)}) collective-permute-start(s16[96,896]{1,0:T(8,128)(2,1)S(1)} %get-tuple-element.66.s2), channel_id=1, source_target_pairs={{0,4},{1,5},{2,6},{3,7},{4,0},{5,1},{6,2},{7,3},{8,12},{9,13},{10,... | collective-permute-start | bytes 516104 | tf_op jit(solution)/shard_map/ppermute | solution.py:45
  105.4 8.2 %collective-permute-start.28 = (s16[96,896]{1,0:T(8,128)(2,1)S(1)}, s16[96,896]{1,0:T(8,128)(2,1)S(1)}, u32[]{:S(2)}, u32[]{:S(2)}) collective-permute-start(s16[96,896]{1,0:T(8,128)(2,1)S(1)} %get-tuple-element.66.s2), channel_id=1, source_target_pairs={{0,2},{1,3},{2,0},{3,1},{4,6},{5,7},{6,4},{7,5},{8,10},{9,11},{10,... | collective-permute-start | bytes 516104 | tf_op jit(solution)/shard_map/ppermute | solution.py:45
  115.0 29.4 %collective-permute-start.31 = (s16[384,896]{1,0:T(8,128)(2,1)S(1)}, s16[384,896]{1,0:T(8,128)(2,1)S(1)}, u32[]{:S(2)}, u32[]{:S(2)}) collective-permute-start(s16[384,896]{1,0:T(8,128)(2,1)S(1)} %shard_map.56), channel_id=1, source_target_pairs={{0,1},{1,0},{2,3},{3,2},{4,5},{5,4},{6,7},{7,6},{8,9},{9,8},{10,11... | collective-permute-start | bytes 2064392 | tf_op jit(solution)/shard_map/ppermute | solution.py:45
  117.3 13.5 %collective-permute-start.32 = (s16[96,896]{1,0:T(8,128)(2,1)S(1)}, s16[96,896]{1,0:T(8,128)(2,1)S(1)}, u32[]{:S(2)}, u32[]{:S(2)}) collective-permute-start(s16[96,896]{1,0:T(8,128)(2,1)S(1)} %get-tuple-element.68), channel_id=1, source_target_pairs={{0,8},{1,9},{2,10},{3,11},{4,12},{5,13},{6,14},{7,15},{8,0},{9,1},... | collective-permute-start | bytes 516104 | tf_op jit(solution)/shard_map/ppermute | solution.py:45
  130.9 8.6 %collective-permute-start.35 = (s16[96,896]{1,0:T(8,128)(2,1)S(1)}, s16[96,896]{1,0:T(8,128)(2,1)S(1)}, u32[]{:S(2)}, u32[]{:S(2)}) collective-permute-start(s16[96,896]{1,0:T(8,128)(2,1)S(1)} %get-tuple-element.70), channel_id=1, source_target_pairs={{0,6},{1,7},{2,4},{3,5},{4,2},{5,3},{6,0},{7,1},{8,14},{9,15},{10,... | collective-permute-start | bytes 516104 | tf_op jit(solution)/shard_map/ppermute | solution.py:45
  132.2 10.5 %collective-permute-start.34 = (s16[96,896]{1,0:T(8,128)(2,1)S(1)}, s16[96,896]{1,0:T(8,128)(2,1)S(1)}, u32[]{:S(2)}, u32[]{:S(2)}) collective-permute-start(s16[96,896]{1,0:T(8,128)(2,1)S(1)} %get-tuple-element.70), channel_id=1, source_target_pairs={{0,4},{1,5},{2,6},{3,7},{4,0},{5,1},{6,2},{7,3},{8,12},{9,13},{10,... | collective-permute-start | bytes 516104 | tf_op jit(solution)/shard_map/ppermute | solution.py:45
  133.3 9.4 %collective-permute-start.33 = (s16[96,896]{1,0:T(8,128)(2,1)S(1)}, s16[96,896]{1,0:T(8,128)(2,1)S(1)}, u32[]{:S(2)}, u32[]{:S(2)}) collective-permute-start(s16[96,896]{1,0:T(8,128)(2,1)S(1)} %get-tuple-element.70), channel_id=1, source_target_pairs={{0,2},{1,3},{2,0},{3,1},{4,6},{5,7},{6,4},{7,5},{8,10},{9,11},{10,... | collective-permute-start | bytes 516104 | tf_op jit(solution)/shard_map/ppermute | solution.py:45
  134.3 9.1 %collective-permute-start.36 = (s16[96,896]{1,0:T(8,128)(2,1)S(1)}, s16[96,896]{1,0:T(8,128)(2,1)S(1)}, u32[]{:S(2)}, u32[]{:S(2)}) collective-permute-start(s16[96,896]{1,0:T(8,128)(2,1)S(1)} %get-tuple-element.70), channel_id=1, source_target_pairs={{0,1},{1,0},{2,3},{3,2},{4,5},{5,4},{6,7},{7,6},{8,9},{9,8},{10,11... | collective-permute-start | bytes 516104 | tf_op jit(solution)/shard_map/ppermute | solution.py:45
  139.6 4.2 %collective-permute-start.39 = (s16[96,896]{1,0:T(8,128)(2,1)S(1)}, s16[96,896]{1,0:T(8,128)(2,1)S(1)}, u32[]{:S(2)}, u32[]{:S(2)}) collective-permute-start(s16[96,896]{1,0:T(8,128)(2,1)S(1)} %collective-permute-done.35.refs_7_), channel_id=1, source_target_pairs={{0,1},{1,0},{2,3},{3,2},{4,5},{5,4},{6,7},{7,6},{8,9},{9,8},{10,11... | collective-permute-start | bytes 516104 | tf_op jit(solution)/shard_map/ppermute | solution.py:45
  142.7 1.4 collective-permute-start.38
  142.7 1.6 %collective-permute-start.37 = (s16[96,896]{1,0:T(8,128)(2,1)S(1)}, s16[96,896]{1,0:T(8,128)(2,1)S(1)}, u32[]{:S(2)}, u32[]{:S(2)}) collective-permute-start(s16[96,896]{1,0:T(8,128)(2,1)S(1)} %collective-permute-done.33.refs_5_), channel_id=1, source_target_pairs={{0,1},{1,0},{2,3},{3,2},{4,5},{5,4},{6,7},{7,6},{8,9},{9,8},{10,11... | collective-permute-start | bytes 516104 | tf_op jit(solution)/shard_map/ppermute | solution.py:45
